TPU v7x, 512 devices: a whole 4x4x16 slice. The times are simulated.
512 devices in a mesh: tm: 128 (over y, z, core), head: 4 (over x).
Axes of the slice: x: 4, y: 4, z: 16, core: 2. Of those that a mesh axis runs over, the one named last changes fastest.
Arguments:
- tokens: bfloat16 [32768, 1024], P('tm'), may hold values from -24 to 24
- q_weight: bfloat16 [1024, 1024], P(None, 'head'), may hold values from -2 to 2
- k_weight: bfloat16 [1024, 1024], P(None, 'head'), may hold values from -2 to 2
- v_weight: bfloat16 [1024, 1024], P(None, 'head'), may hold values from -0.1875 to 0.1875
- o_weight: bfloat16 [1024, 1024], P('head'), may hold values from -0.1875 to 0.1875
- rand_blocks: int32 [256, 3], P('tm'), may hold values from 0 to 255, as said below
- global_pos: int32 [256], replicated, may hold values from 0 to 32767, as said below
Outputs:
- mixed_out: bfloat16 [32768, 1024], P(('tm', 'head'))
Inputs may be any that keep to these rules, and one draw needn't show every extreme that they name: rand_blocks[b, r] names a block whose shard index (block // 2) differs from that of b by at most 2; in every draw some entry differs by exactly 2. `global_pos`: 256 distinct positions in ascending order.
All inputs are finite; a program needn't handle non-finite values.
Results may differ from a plain program's by a relative error of at most 0.011.
Values may be sent and summed in bfloat16 or wider, within the bound.
A program may use at most 64 MiB of HBM per device.

v0:
```python
import jax
import jax.numpy as jnp
from jax import lax
from jax.sharding import PartitionSpec as P

HEAD_DIM = 64
BLOCK = 128
GLOBALS = 256
RAND = 3
SPREAD = 2


def shifted(block, axis, distance):
    devices = range(lax.axis_size(axis))
    route = [(i - distance, i) for i in devices if i - distance in devices]
    return lax.ppermute(block, axis, route)


def shards(tokens, q_weight, k_weight, v_weight, o_weight, rand_blocks, global_pos):
    tok_rows = tokens.shape[0]
    feats = q_weight.shape[1]
    heads_here = feats // HEAD_DIM
    per_shard = tok_rows // BLOCK
    shard_count = lax.axis_size("tm")
    shard_index = lax.axis_index("tm")
    score_scale = HEAD_DIM ** (-0.5)
    queries = jnp.dot(tokens, q_weight, preferred_element_type=jnp.float32).astype(jnp.bfloat16)
    keys_here = jnp.dot(tokens, k_weight, preferred_element_type=jnp.float32).astype(jnp.bfloat16)
    values_here = jnp.dot(tokens, v_weight, preferred_element_type=jnp.float32).astype(jnp.bfloat16)
    key_value = jnp.concatenate([keys_here, values_here], axis=1)
    positions = shard_index * tok_rows + jnp.arange(tok_rows, dtype=jnp.int32)
    picked = global_pos[:, None] == positions[None, :]
    pick_table = picked.astype(jnp.bfloat16)
    projected = jnp.concatenate([queries, key_value], axis=1)
    summed_rows = lax.psum(
        jnp.dot(pick_table, projected, preferred_element_type=jnp.float32), "tm"
    ).astype(jnp.bfloat16)
    global_q = summed_rows[:, :feats]
    global_k = summed_rows[:, feats : 2 * feats]
    global_v = summed_rows[:, 2 * feats :]
    earlier = []
    moving = key_value
    for hop_number in range(SPREAD):
        moving = shifted(moving, "tm", 1)
        earlier = [moving] + earlier
    later_keys = []
    moving = key_value
    for hop_number in range(SPREAD):
        moving = shifted(moving, "tm", -1)
        later_keys = later_keys + [moving]
    extended = jnp.concatenate(earlier + [key_value] + later_keys, axis=0).reshape(
        -1, BLOCK, 2 * feats
    )
    own_first = SPREAD * per_shard
    window = jnp.stack(
        [
            extended[own_first + shift_by : own_first + shift_by + per_shard]
            for shift_by in (-2, -1, 0, 1)
        ],
        axis=1,
    )
    chosen = extended[rand_blocks - (shard_index - SPREAD) * per_shard]
    gathered_keys = jnp.concatenate([window, chosen], axis=1).reshape(per_shard, -1, 2 * feats)
    key_length = gathered_keys.shape[1]
    block_ids = (
        shard_index * per_shard
        + jnp.arange(per_shard, dtype=jnp.int32)[:, None]
        + jnp.arange(-2, 2, dtype=jnp.int32)[None, :]
    )
    inside = (block_ids >= 0) & (block_ids < shard_count * per_shard)
    valid_keys = jnp.concatenate(
        [jnp.repeat(inside, BLOCK, axis=1), jnp.ones((per_shard, RAND * BLOCK), dtype=bool)], axis=1
    )
    block_q = queries.reshape(per_shard, BLOCK, heads_here, HEAD_DIM)
    near_k = gathered_keys[:, :, :feats].reshape(per_shard, key_length, heads_here, HEAD_DIM)
    near_v = gathered_keys[:, :, feats:].reshape(per_shard, key_length, heads_here, HEAD_DIM)
    glob_k4 = global_k.reshape(GLOBALS, heads_here, HEAD_DIM)
    glob_v4 = global_v.reshape(GLOBALS, heads_here, HEAD_DIM)
    near_scores = (
        jnp.einsum("jqhd,jkhd->jhqk", block_q, near_k, preferred_element_type=jnp.float32)
        * score_scale
    )
    near_scores = jnp.where(valid_keys[:, None, None, :], near_scores, -jnp.inf)
    far_scores = (
        jnp.einsum("jqhd,ghd->jhqg", block_q, glob_k4, preferred_element_type=jnp.float32)
        * score_scale
    )
    row_max = jnp.maximum(jnp.max(near_scores, axis=3), jnp.max(far_scores, axis=3))
    near_exp = jnp.exp(near_scores - row_max[..., None])
    far_exp = jnp.exp(far_scores - row_max[..., None])
    denominator = jnp.sum(near_exp, axis=3) + jnp.sum(far_exp, axis=3)
    numerator = jnp.einsum(
        "jhqk,jkhd->jqhd", near_exp.astype(jnp.bfloat16), near_v, preferred_element_type=jnp.float32
    )
    numerator = numerator + jnp.einsum(
        "jhqg,ghd->jqhd", far_exp.astype(jnp.bfloat16), glob_v4, preferred_element_type=jnp.float32
    )
    local_out = (
        (numerator / jnp.transpose(denominator, (0, 2, 1))[..., None])
        .astype(jnp.bfloat16)
        .reshape(tok_rows, feats)
    )
    glob_q4 = global_q.reshape(GLOBALS, heads_here, HEAD_DIM)
    local_k4 = keys_here.reshape(tok_rows, heads_here, HEAD_DIM)
    glob_scores = (
        jnp.einsum("ghd,thd->hgt", glob_q4, local_k4, preferred_element_type=jnp.float32)
        * score_scale
    )
    local_max = jnp.max(glob_scores, axis=2)
    glob_exp = jnp.exp(glob_scores - local_max[..., None])
    local_totals = jnp.sum(glob_exp, axis=2)
    local_values = values_here.astype(jnp.float32).reshape(tok_rows, heads_here, HEAD_DIM)
    local_accum = jnp.einsum(
        "hgt,thd->hgd", glob_exp, local_values, precision=lax.Precision.HIGHEST
    )
    peak = lax.pmax(local_max, "tm")
    rescale = jnp.exp(local_max - peak)
    totals, accumulated = lax.psum((local_totals * rescale, local_accum * rescale[..., None]), "tm")
    global_out = (accumulated / totals[..., None]).astype(jnp.bfloat16)
    global_out = jnp.transpose(global_out, (1, 0, 2)).reshape(GLOBALS, feats)
    placed = jnp.einsum(
        "gt,gf->tf", pick_table, global_out, preferred_element_type=jnp.float32
    ).astype(jnp.bfloat16)
    is_global = jnp.any(picked, axis=0)
    attended = jnp.where(is_global[:, None], placed, local_out)
    mixed_out = lax.psum_scatter(
        jnp.dot(attended, o_weight, preferred_element_type=jnp.float32),
        "head",
        scatter_dimension=0,
        tiled=True,
    )
    return mixed_out.astype(jnp.bfloat16)


def solution(mesh):
    placed = (
        P("tm", None),
        P(None, "head"),
        P(None, "head"),
        P(None, "head"),
        P("head", None),
        P("tm", None),
        P(),
    )
    return jax.shard_map(
        shards, mesh=mesh, in_specs=placed, out_specs=P(("tm", "head"), None), check_vma=False
    )
```

profile of v0, /device:TPU:1, one launch (start us, length us, event | category | flops | bytes accessed | tf_op | source)
XLA Modules:
  0.0 1165.6 jit_solution(3396608173455110699)
XLA Ops:
  6.5 0.0 all-reduce.4.cloned.1.call-start
  6.6 1.7 convolution_convert_fusion
  8.2 1.6 convolution_convert_fusion.1
  9.8 4.9 collective-permute-start
  14.8 5.1 collective-permute-start.1
  19.9 0.4 convolution_convert_fusion.2
  20.3 0.3 fusion.20
  20.6 498.9 %all-reduce.5 = bf16[256,768]{1,0:T(8,128)(2,1)S(1)} all-reduce(f32[256,768]{1,0:T(8,128)S(1)} %fusion.20), channel_id=1, replica_groups=mesh['tm'=128,'head'=4] {'tm'}, use_global_device_ids=true, to_apply=%region_1.2 | all-reduce | flops 196608 | bytes 1179648 | tf_op jit(solution)/shard_map/psum | solution.py:35
  519.6 0.1 copy.76
  519.7 0.4 fusion.45
  520.1 0.0 copy-start.10
  520.1 251.8 %pmax.7 = f32[4,256]{1,0:T(4,128)S(1)} all-reduce(f32[4,256]{1,0:T(4,128)S(1)} %get-tuple-element.21), channel_id=1, replica_groups=mesh['tm'=128,'head'=4] {'tm'}, use_global_device_ids=true, to_apply=%region_3.4 | all-reduce | flops 1024 | bytes 8192 | tf_op jit(solution)/shard_map/pmax | solution.py:116
  771.9 0.2 fusion.15
  772.1 1.3 convolution_multiply_fusion.2
  773.4 0.0 all-reduce.4.cloned.1.call-update
  773.4 0.0 reduce-scatter.2.cloned.1.call-start
  773.6 0.1 copy.86
  773.7 0.1 compare_and_fusion
  773.8 0.4 fusion.44
  774.1 0.1 broadcast_bitcast_fusion
  774.2 0.6 compare_reduce_fusion
  774.8 0.1 reshape.87
  774.9 0.1 copy.100
  775.1 0.8 copy.89
  775.9 246.9 %psum.23 = f32[4,256]{1,0:T(4,128)S(1)} all-reduce(f32[4,256]{1,0:T(4,128)S(1)} %get-tuple-element.5), channel_id=1, replica_groups=mesh['tm'=128,'head'=4] {'tm'}, use_global_device_ids=true, to_apply=%region_6.7 | all-reduce | flops 1024 | bytes 8192 | tf_op jit(solution)/shard_map/psum | solution.py:118
  1022.7 0.0 collective-permute-done
  1022.7 1.9 collective-permute-start.2
  1024.7 72.1 %all-reduce.4.cloned.1.call-done = f32[4,256,64]{1,2,0:T(8,128)} async-done(((f32[4,256,64]{1,2,0:T(8,128)}), f32[4,256,64]{1,2,0:T(8,128)}) %all-reduce.4.cloned.1.call-update) | async-done | bytes 262160 | tf_op jit(solution)/shard_map/psum | solution.py:118
  1096.8 1.6 divide_convert_fusion
  1098.4 0.1 copy.98
  1098.5 0.0 collective-permute-done.1
  1098.5 3.9 collective-permute-start.3
  1102.4 0.7 constant_dynamic-update-slice_fusion.9
  1103.1 0.7 constant_dynamic-update-slice_fusion.4
  1103.9 0.8 constant_dynamic-update-slice_fusion.3
  1104.6 0.7 constant_dynamic-update-slice_fusion.2
  1105.4 1.8 constant_dynamic-update-slice_fusion.1
  1107.2 0.9 copy.99
  1108.0 0.1 copy.101
  1108.2 0.0 collective-permute-done.3
  1108.2 0.7 constant_dynamic-update-slice_fusion
  1108.9 1.6 copy.78
  1110.6 1.7 constant_dynamic-update-slice_fusion.8
  1112.2 0.7 constant_dynamic-update-slice_fusion.7
  1113.0 0.7 constant_dynamic-update-slice_fusion.6
  1113.7 1.5 gather_fusion
  1115.2 2.1 constant_dynamic-update-slice_fusion.5
  1117.3 2.5 fusion.42
  1119.8 1.5 copy.84
  1121.3 0.8 fusion
  1122.2 0.9 fusion.1
  1123.1 0.8 copy-done.1
  1123.9 0.6 copy.83
  1124.5 0.0 copy-start.5
  1124.5 3.1 fusion.9
  1127.7 0.2 fusion.16
  1127.9 0.2 fusion.12
  1128.1 0.2 copy.103
  1128.3 0.2 reshape.97
  1128.5 0.0 copy-done.3
  1128.6 1.6 fusion.14
  1130.2 0.0 reduce-scatter.2.cloned.1.call-update
  1130.2 27.0 %reduce-scatter.2.cloned.1.call-done = f32[64,1024]{1,0:T(8,128)} async-done(((f32[256,1024]{1,0:T(8,128)}), f32[64,1024]{1,0:T(8,128)}) %reduce-scatter.2.cloned.1.call-update) | async-done | bytes 262160 | tf_op jit(solution)/shard_map/reduce_scatter | solution.py:126
  1157.1 1.6 convert_element_type.41
  (33 shorter events, 0.2 us)
Async XLA Ops:
  6.5 1122.0 %copy-start = (bf16[256,1024]{1,0:T(8,128)(2,1)S(1)}, bf16[256,1024]{1,0:T(8,128)(2,1)}, u32[]{:S(2)}) copy-start(bf16[256,1024]{1,0:T(8,128)(2,1)} %param.11) | copy-start | bytes 1572868
  6.5 13.4 %copy-start.2 = (bf16[256,1024]{1,0:T(8,128)(2,1)S(1)}, bf16[256,1024]{1,0:T(8,128)(2,1)}, u32[]{:S(2)}) copy-start(bf16[256,1024]{1,0:T(8,128)(2,1)} %param.7) | copy-start | bytes 1572868
  6.5 13.4 %copy-start.4 = (bf16[1024,256]{1,0:T(8,128)(2,1)S(1)}, bf16[1024,256]{1,0:T(8,128)(2,1)}, u32[]{:S(2)}) copy-start(bf16[1024,256]{1,0:T(8,128)(2,1)} %param.8) | copy-start | bytes 1572868
  6.5 13.8 %copy-start.6 = (s32[256]{0:T(256)S(1)}, s32[256]{0:T(256)}, u32[]{:S(2)}) copy-start(s32[256]{0:T(256)} %param.13) | copy-start | bytes 3076
  6.5 1090.2 %all-reduce.4.cloned.1.call-start = ((), (), s32[]{:S(2)}) async-start(), calls=%async_computation.1 | async-start | bytes 524288 | tf_op jit(solution)/shard_map/psum | solution.py:118
  9.8 1012.9 %collective-permute-start = (bf16[256,512]{0,1:T(8,128)(2,1)S(1)}, bf16[256,512]{0,1:T(8,128)(2,1)S(1)}, u32[]{:S(2)}, u32[]{:S(2)}) collective-permute-start(bf16[256,512]{0,1:T(8,128)(2,1)S(1)} %pad_maximum_fusion.4), channel_id=1, source_target_pairs={{0,4},{4,8},{8,12},{12,16},{16,20},{20,24},{24,28},{28,32},{32,36}... | collective-permute-start | bytes 786440 | tf_op jit(solution)/shard_map/ppermute | solution.py:16
  14.8 1083.8 %collective-permute-start.1 = (bf16[256,512]{0,1:T(8,128)(2,1)S(1)}, bf16[256,512]{0,1:T(8,128)(2,1)}, u32[]{:S(2)}, u32[]{:S(2)}) collective-permute-start(bf16[256,512]{0,1:T(8,128)(2,1)S(1)} %pad_maximum_fusion.4), channel_id=1, source_target_pairs={{4,0},{8,4},{12,8},{16,12},{20,16},{24,20},{28,24},{32,28},{36,32}... | collective-permute-start | bytes 786440 | tf_op jit(solution)/shard_map/ppermute | solution.py:16
  19.9 754.3 %copy-start.7 = (s32[256]{0:T(256)}, s32[256]{0:T(256)S(1)}, u32[]{:S(2)}) copy-start(s32[256]{0:T(256)S(1)} %iota_add_fusion) | copy-start | bytes 3076
  520.1 253.6 %copy-start.10 = (s32[2,3]{1,0:T(2,128)S(1)}, s32[2,3]{1,0:T(2,128)}, u32[]{:S(2)}) copy-start(s32[2,3]{1,0:T(2,128)} %param.12) | copy-start | bytes 76
  773.4 383.7 %reduce-scatter.2.cloned.1.call-start = ((), (), s32[]{:S(2)}) async-start(), calls=%async_computation.2 | async-start | bytes 1310720 | tf_op jit(solution)/shard_map/reduce_scatter | solution.py:126
  1022.7 80.4 %collective-permute-start.2 = (bf16[256,512]{0,1:T(8,128)(2,1)S(1)}, bf16[256,512]{0,1:T(8,128)(2,1)S(1)}, u32[]{:S(2)}, u32[]{:S(2)}) collective-permute-start(bf16[256,512]{0,1:T(8,128)(2,1)S(1)} %collective-permute-done), channel_id=1, source_target_pairs={{0,4},{4,8},{8,12},{12,16},{16,20},{20,24},{24,28},{28,32},{32,36}... | collective-permute-start | bytes 786440 | tf_op jit(solution)/shard_map/ppermute | solution.py:16
  1098.5 9.7 collective-permute-start.3
  1122.1 1.8 copy-start.1
  1124.5 3.4 copy-start.5
  1127.6 0.9 copy-start.3
  1127.7 0.9 copy-start.8
  1127.7 0.9 copy-start.9
Sparse Core Ops, SparseCore 0:
  773.6 323.1 all-reduce.3
  1130.3 26.7 reduce-scatter.1
where the time goes:
time: 1170 us
  blocking collectives  998 us (85%)
  waiting for transfers between devices  99.1 us (8%)
  local copies, waits for them, and re-layouts  19.7 us (2%)
  starting transfers between devices  15.9 us (1%)
  between operations  13.8 us (1%)
    psum x1, blocking collectives, shards(): lax.psum(jnp.dot(pick_table, projected, preferred_element_type=jnp.float3...  499 us
    pmax x1, blocking collectives, shards(): peak = lax.pmax(local_max, 'tm')  252 us
    psum x1, blocking collectives, shards(): lax.psum((local_totals * rescale, local_accum * rescale[..., None]), 'tm')  247 us
    psum x1, waiting for transfers between devices, shards(): lax.psum((local_totals * rescale, local_accum * rescale[..., None]), 'tm')  72.1 us
    reduce_scatter x1, waiting for transfers between devices, shards(): lax.psum_scatter(jnp.dot(attended, o_weight, preferred_element_type=jnp.f...  27 us
  transfers between devices with their start and end apart: 6, of which 2 were waited for; matrix products, arithmetic and copies ran while one was open for 1% of the time, Pallas kernels for 0%

commit v1 on v0

v1 whole, which is shorter than its diff:
```python
import functools
import math

import jax
import jax.numpy as jnp
from jax import lax
from jax.experimental import pallas as pl
from jax.experimental.pallas import tpu as pltpu
from jax.sharding import PartitionSpec as P

HEAD_DIM = 64
BLOCK = 128
GLOBALS = 256
RAND = 3
SPREAD = 2
TOK = 256
FEATS = 256
HEADS_HERE = FEATS // HEAD_DIM
LOG2_SCALE = math.log2(math.e) / math.sqrt(HEAD_DIM)
NEG = -1e30
MESH = pl.DeviceIdType.MESH
F32 = jnp.float32
BF16 = jnp.bfloat16


def dot_nn(a, b):
    return jnp.dot(a, b, preferred_element_type=F32)


def dot_nt(a, b):
    return lax.dot_general(a, b, (((1,), (1,)), ((), ())), preferred_element_type=F32)


def split_of(shards):
    return {128: (4, 4, 4), 16: (2, 2, 2), 64: (4, 2, 4)}[shards]


def scratch_of(split, heads, d):
    y_n, zn_n, zf_n = split
    r = 2 * y_n
    ch = GLOBALS // r
    vm = pltpu.VMEM

    def stream(tag, width):
        return {
            tag + "part": vm((GLOBALS, width), BF16),
            tag + "a": vm((r - 1, ch, width), BF16),
            tag + "bs": vm((ch, width), BF16),
            tag + "b": vm((zn_n - 1, ch, width), BF16),
            tag + "cs": vm((ch, width), BF16),
            tag + "c": vm((zf_n - 1, ch, width), BF16),
            tag + "full": vm((GLOBALS, width), BF16),
        }

    out = {
        "tok": vm((TOK, d), BF16),
        "wq": vm((d, FEATS), BF16),
        "wk": vm((d, FEATS), BF16),
        "wv": vm((d, FEATS), BF16),
        "osl": vm((heads, FEATS, d), BF16),
        "asl": vm((heads - 1, TOK // heads, FEATS), BF16),
        "att": vm((TOK, FEATS), BF16),
        "attl": vm((TOK, FEATS), F32),
        "att_t": vm((FEATS, TOK), F32),
        "q": vm((TOK, FEATS), BF16),
        "kx": vm((10, BLOCK, FEATS), BF16),
        "vx": vm((10, FEATS, BLOCK), BF16),
        "gvt": vm((2, FEATS, BLOCK), BF16),
        "s": vm((9, BLOCK, 2 * BLOCK), F32),
        "pick": vm((TOK, GLOBALS), BF16),
        "lpart": vm((HEADS_HERE, 1, GLOBALS), F32),
        "la": vm((r - 1, 1, GLOBALS), F32),
        "lbs": vm((1, 1, GLOBALS), F32),
        "lb": vm((zn_n - 1, 1, GLOBALS), F32),
        "lcs": vm((1, 1, GLOBALS), F32),
        "lc": vm((zf_n - 1, 1, GLOBALS), F32),
    }
    out.update(stream("q_", FEATS))
    out.update(stream("kv_", 2 * FEATS))
    out.update(stream("o_", GLOBALS))
    copies = 3 * (2 * (r - 1) + zn_n + zf_n - 2) + (r - 1 + zn_n + zf_n - 2) + 8 + 2 * (heads - 1)
    out["send"] = pltpu.SemaphoreType.DMA((copies,))
    out["recv"] = pltpu.SemaphoreType.DMA((copies,))
    out["load"] = pltpu.SemaphoreType.DMA((5,))
    return out


def kernel(split, heads, names, tok_h, wq_h, wk_h, wv_h, ow_h, rand_s, grow_v, out_v, *scratch):
    m = dict(zip(names, scratch))
    y_n, zn_n, zf_n = split
    r = 2 * y_n
    ch = GLOBALS // r
    shards = r * zn_n * zf_n
    tm = lax.axis_index("tm")
    hd = lax.axis_index("head")
    z_n = zn_n * zf_n
    y = tm // (2 * z_n)
    z = (tm // 2) % z_n
    c = tm % 2
    j = y * 2 + c
    zn = z % zn_n
    zf = z // zn_n

    def dev_j(jj):
        return ((jj // 2) * (2 * z_n) + z * 2 + jj % 2, hd)

    def dev_z(zz):
        return (y * (2 * z_n) + zz * 2 + c, hd)

    group_j = [dev_j((j + d) % r) for d in range(1, r)]
    group_n = [dev_z(zf * zn_n + (zn + d) % zn_n) for d in range(1, zn_n)]
    group_f = [dev_z(((zf + d) % zf_n) * zn_n + zn) for d in range(1, zf_n)]
    group_h = [(tm, (hd + d) % heads) for d in range(1, heads)]
    steps_w = (1, -1, 2, -2)
    group_w = [((tm + d + shards) % shards, hd) for d in steps_w]
    everyone = group_j + group_n + group_f + group_h + group_w

    loads = [
        pltpu.make_async_copy(src, m[dst], m["load"].at[i])
        for i, (src, dst) in enumerate(
            ((tok_h, "tok"), (wq_h, "wq"), (wk_h, "wk"), (wv_h, "wv"))
        )
    ]
    loads.append(pltpu.make_async_copy(ow_h, m["osl"].at[0], m["load"].at[4]))
    for copy in loads:
        copy.start()

    barrier = pltpu.get_barrier_semaphore()
    for dev in everyone:
        pl.semaphore_signal(barrier, inc=1, device_id=dev, device_id_type=MESH)

    count = [0]
    started = []

    def send(src, dst, dev):
        n = count[0]
        count[0] += 1
        copy = pltpu.make_async_remote_copy(
            src_ref=src,
            dst_ref=dst,
            send_sem=m["send"].at[n],
            recv_sem=m["recv"].at[n],
            device_id=dev,
            device_id_type=MESH,
        )
        copy.start()
        started.append(copy)
        return copy

    def rows(jj):
        return pl.ds(pl.multiple_of(jj * ch, ch), ch)

    def start_a(tag):
        part = m[tag + "part"]
        return [
            send(part.at[rows((j + d) % r)], m[tag + "a"].at[d - 1], group_j[d - 1])
            for d in range(1, r)
        ]

    def gather(first, copies, slots):
        total = first.astype(F32)
        for n, copy in enumerate(copies):
            copy.wait_recv()
            total = total + slots[n].astype(F32)
        return total.astype(BF16)

    def start_b(tag):
        return [send(m[tag + "bs"], m[tag + "b"].at[d], group_n[d]) for d in range(zn_n - 1)]

    def start_c(tag):
        return [send(m[tag + "cs"], m[tag + "c"].at[d], group_f[d]) for d in range(zf_n - 1)]

    def start_d(tag):
        mine = m[tag + "full"].at[rows(j)]
        return [send(mine, mine, group_j[d]) for d in range(r - 1)]

    loads[0].wait()
    loads[1].wait()
    q = dot_nn(m["tok"][...], m["wq"][...]).astype(BF16)
    m["q"][...] = q
    spots = lax.broadcasted_iota(jnp.int32, (TOK, GLOBALS), 0) + tm * TOK
    pick = jnp.where(spots == grow_v[...], 1.0, 0.0).astype(F32)
    m["pick"][...] = pick.astype(BF16)
    pick_t = pick.T.astype(BF16)
    m["q_part"][...] = dot_nn(pick_t, q).astype(BF16)
    pl.semaphore_wait(barrier, len(everyone))
    qa = start_a("q_")

    loads[4].wait()
    ow = [send(m["osl"].at[0], m["osl"].at[d + 1], group_h[d]) for d in range(heads - 1)]

    loads[2].wait()
    k = dot_nn(m["tok"][...], m["wk"][...]).astype(BF16)
    m["kv_part"][:, :FEATS] = dot_nn(pick_t, k).astype(BF16)
    for b in range(2):
        m["kx"][4 + b] = k[b * BLOCK : (b + 1) * BLOCK]
    loads[3].wait()
    v32 = dot_nn(m["tok"][...], m["wv"][...])
    m["kv_part"][:, FEATS:] = dot_nn(pick_t, v32.astype(BF16)).astype(BF16)
    kva = start_a("kv_")
    v_t = v32.T.astype(BF16)
    for b in range(2):
        m["vx"][4 + b] = v_t[:, b * BLOCK : (b + 1) * BLOCK]

    m["q_bs"][...] = gather(m["q_part"][rows(j)], qa, m["q_a"])
    qb = start_b("q_")
    m["kv_bs"][...] = gather(m["kv_part"][rows(j)], kva, m["kv_a"])
    kvb = start_b("kv_")
    m["q_cs"][...] = gather(m["q_bs"][...], qb, m["q_b"])
    qc = start_c("q_")
    m["kv_cs"][...] = gather(m["kv_bs"][...], kvb, m["kv_b"])
    kvc = start_c("kv_")

    window = []
    for step, dev in zip(steps_w, group_w):
        slot = 2 * (SPREAD - step)
        for name in ("kx", "vx"):
            window.append(send(m[name].at[pl.ds(4, 2)], m[name].at[pl.ds(slot, 2)], dev))

    m["q_full"][rows(j)] = gather(m["q_cs"][...], qc, m["q_c"])
    qd = start_d("q_")

    lane_head = lax.broadcasted_iota(jnp.int32, (1, FEATS), 1) // HEAD_DIM

    def head_mask(h):
        return jnp.where(lane_head == h, 1.0, 0.0).astype(BF16)

    for copy in qd:
        copy.wait_recv()
    gq = m["q_full"][...]
    for h in range(HEADS_HERE):
        gq_h = gq * head_mask(h)
        s0 = dot_nt(m["kx"][4], gq_h) * LOG2_SCALE
        s1 = dot_nt(m["kx"][5], gq_h) * LOG2_SCALE
        peak = jnp.maximum(jnp.max(s0, axis=0, keepdims=True), jnp.max(s1, axis=0, keepdims=True))
        p0 = jnp.exp2(s0 - peak)
        p1 = jnp.exp2(s1 - peak)
        total = jnp.sum(p0, axis=0, keepdims=True) + jnp.sum(p1, axis=0, keepdims=True)
        feats = pl.ds(h * HEAD_DIM, HEAD_DIM)
        acc = dot_nn(m["vx"][4, feats, :], p0.astype(BF16))
        acc = acc + dot_nn(m["vx"][5, feats, :], p1.astype(BF16))
        m["o_part"][feats, :] = (acc / total).astype(BF16)
        m["lpart"][h] = peak + jnp.log2(total)

    def head_of(jj):
        return (jj * HEADS_HERE) // r

    oa = start_a("o_")
    la = [
        send(m["lpart"].at[head_of((j + d) % r)], m["la"].at[d - 1], group_j[d - 1])
        for d in range(1, r)
    ]

    def combine(o_first, l_first, o_copies, l_copies, o_slots, l_slots):
        for copy in o_copies + l_copies:
            copy.wait_recv()
        size = len(o_copies)
        logs = [l_first] + [l_slots[n] for n in range(size)]
        peak = functools.reduce(jnp.maximum, logs)
        shares = [jnp.exp2(x - peak) for x in logs]
        total = functools.reduce(jnp.add, shares)
        acc = o_first.astype(F32) * shares[0]
        for n in range(size):
            acc = acc + o_slots[n].astype(F32) * shares[n + 1]
        return (acc / total).astype(BF16), peak + jnp.log2(total)

    o, l = combine(m["o_part"][rows(j)], m["lpart"][head_of(j)], oa, la, m["o_a"], m["la"])
    m["o_bs"][...] = o
    m["lbs"][0] = l
    ob = start_b("o_")
    lb = [send(m["lbs"].at[0], m["lb"].at[d], group_n[d]) for d in range(zn_n - 1)]

    m["kv_full"][rows(j)] = gather(m["kv_cs"][...], kvc, m["kv_c"])
    kvd = start_d("kv_")

    o, l = combine(m["o_bs"][...], m["lbs"][0], ob, lb, m["o_b"], m["lb"])
    m["o_cs"][...] = o
    m["lcs"][0] = l
    oc = start_c("o_")
    lc = [send(m["lcs"].at[0], m["lc"].at[d], group_f[d]) for d in range(zf_n - 1)]

    for copy in kvd + window:
        copy.wait_recv()
    gv_t = m["kv_full"][:, FEATS:].astype(F32).T.astype(BF16)
    for b in range(2):
        m["gvt"][b] = gv_t[:, b * BLOCK : (b + 1) * BLOCK]
    blocks = 2 * shards

    def attend(step, carry):
        jb = step // 2
        pair = step % 2
        qb_here = m["q"][pl.ds(pl.multiple_of(jb * BLOCK, BLOCK), BLOCK), :]
        q2 = jnp.concatenate(
            [qb_here * head_mask(2 * pair), qb_here * head_mask(2 * pair + 1)], axis=0
        )
        feats = pl.ds(pl.multiple_of(pair * 2 * HEAD_DIM, 2 * HEAD_DIM), 2 * HEAD_DIM)
        spots_x = [2 + jb + w for w in range(4)]
        spots_x += [jnp.clip(rand_s[jb, n] - 2 * tm + 2 * SPREAD, 0, 9) for n in range(RAND)]
        peak = None
        for n in range(9):
            if n < 7:
                keys = m["kx"][spots_x[n]]
            else:
                keys = m["kv_full"][pl.ds((n - 7) * BLOCK, BLOCK), :FEATS]
            s = dot_nt(keys, q2) * LOG2_SCALE
            if n in (0, 1, 3):
                block = 2 * tm + jb + n - 2
                inside = (block >= 0) & (block < blocks)
                s = jnp.where(inside, s, NEG)
            m["s"][n] = s
            top = jnp.max(s, axis=0, keepdims=True)
            peak = top if peak is None else jnp.maximum(peak, top)
        total = jnp.zeros((1, 2 * BLOCK), F32)
        acc = jnp.zeros((2 * HEAD_DIM, 2 * BLOCK), F32)
        for n in range(9):
            e = jnp.exp2(m["s"][n] - peak)
            total = total + jnp.sum(e, axis=0, keepdims=True)
            if n < 7:
                values = m["vx"][spots_x[n], feats, :]
            else:
                values = m["gvt"][n - 7, feats, :]
            acc = acc + dot_nn(values, e.astype(BF16))
        acc = acc / total
        lanes = pl.ds(pl.multiple_of(jb * BLOCK, BLOCK), BLOCK)
        for n in range(2):
            here = pl.ds(pl.multiple_of(pair * 2 * HEAD_DIM + n * HEAD_DIM, HEAD_DIM), HEAD_DIM)
            m["att_t"][here, lanes] = acc[
                n * HEAD_DIM : (n + 1) * HEAD_DIM, n * BLOCK : (n + 1) * BLOCK
            ]
        return carry

    lax.fori_loop(0, 4, attend, 0)
    is_global = jnp.max(m["pick"][...].astype(F32), axis=1, keepdims=True)
    m["attl"][...] = jnp.where(is_global > 0.5, 0.0, m["att_t"][...].T)

    o, l = combine(m["o_cs"][...], m["lcs"][0], oc, lc, m["o_c"], m["lc"])
    m["o_full"][rows(j)] = o
    od = start_d("o_")
    for copy in od:
        copy.wait_recv()

    placed = dot_nt(m["pick"][...], m["o_full"][...])
    m["att"][...] = (placed + m["attl"][...]).astype(BF16)
    per = TOK // heads

    def out_rows(hh):
        return pl.ds(pl.multiple_of(hh * per, per), per)

    ax = [
        send(m["att"].at[out_rows((hd + d + 1) % heads)], m["asl"].at[d], group_h[d])
        for d in range(heads - 1)
    ]
    mixed = dot_nn(m["att"][out_rows(hd)], m["osl"][0])
    for d in range(heads - 1):
        ow[d].wait_recv()
        ax[d].wait_recv()
        mixed = mixed + dot_nn(m["asl"][d], m["osl"][d + 1])
    out_v[...] = mixed.astype(BF16)
    for copy in started:
        copy.wait_send()


def shards_fn(tokens, q_weight, k_weight, v_weight, o_weight, rand_blocks, global_pos):
    shards = lax.axis_size("tm")
    heads = lax.axis_size("head")
    split = split_of(shards)
    d = tokens.shape[1]
    scratch = scratch_of(split, heads, d)
    hbm = pl.BlockSpec(memory_space=pl.ANY)
    return pl.pallas_call(
        functools.partial(kernel, split, heads, list(scratch)),
        out_shape=jax.ShapeDtypeStruct((TOK // heads, d), BF16),
        in_specs=[hbm] * 5
        + [
            pl.BlockSpec(memory_space=pltpu.SMEM),
            pl.BlockSpec(memory_space=pltpu.VMEM),
        ],
        out_specs=pl.BlockSpec(memory_space=pltpu.VMEM),
        scratch_shapes=list(scratch.values()),
        compiler_params=pltpu.CompilerParams(
            collective_id=0, has_side_effects=True, vmem_limit_bytes=48 << 20
        ),
        name="layer",
    )(
        tokens,
        q_weight,
        k_weight,
        v_weight,
        o_weight,
        rand_blocks,
        global_pos.reshape(1, GLOBALS),
    )


def solution(mesh):
    placed = (
        P("tm", None),
        P(None, "head"),
        P(None, "head"),
        P(None, "head"),
        P("head", None),
        P("tm", None),
        P(),
    )
    return jax.shard_map(
        shards_fn, mesh=mesh, in_specs=placed, out_specs=P(("tm", "head"), None), check_vma=False
    )
```

time: 1170 us -> 81.3 us (0.07)
  blocking collectives: 998 us -> 0 us
  waiting for transfers between devices: 99.1 us -> 0 us
  Pallas kernels: 0 us -> 73.7 us
  starting transfers between devices: 15.9 us -> 0 us
  between operations: 13.8 us -> 0.02 us
  local copies, waits for them, and re-layouts: 19.7 us -> 7.22 us
    psum x2 -> x0, blocking collectives: 746 us -> none  [the longest x1 499 us: shards(): lax.psum(jnp.dot(pick_table, projected, preferred_element_type=jnp.float3...]
    pmax x1 -> x0, blocking collectives: 252 us -> none  [shards(): peak = lax.pmax(local_max, 'tm')]
    pallas_call x0 -> x1, Pallas kernels: none -> 73.7 us  [shards_fn(): pl.pallas_call(functools.partial(kernel, split, heads, list(scratch)), ou...]
    psum x1 -> x0, waiting for transfers between devices: 72.1 us -> none  [shards(): lax.psum((local_totals * rescale, local_accum * rescale[..., None]), 'tm')]
    reduce_scatter x1 -> x0, waiting for transfers between devices: 27 us -> none  [shards(): lax.psum_scatter(jnp.dot(attended, o_weight, preferred_element_type=jnp.f...]
    ppermute x4 -> x0, starting transfers between devices: 15.8 us -> none  [shifted(): return lax.ppermute(block, axis, route)]
  transfers between devices with their start and end apart: 6 -> 0, of which waited for: 2 -> 0; matrix products, arithmetic and copies ran while one was open for 1% -> 0% of each run, Pallas kernels for 0% -> 0%
where the time goes in v1:
time: 81.3 us; the launch traced here: 81 us
  Pallas kernels  73.7 us (91%)
  local copies, waits for them, and re-layouts  7.22 us (9%)
    pallas_call x1, Pallas kernels, shards_fn(): pl.pallas_call(functools.partial(kernel, split, heads, list(scratch)), ou...  73.7 us
    unnamed x15, local copies, waits for them, and re-layouts  7.22 us

profile of v1, /device:TPU:1, one launch (start us, length us, event | category | flops | bytes accessed | tf_op | source)
XLA Modules:
  0.0 81.0 jit_solution(669230533294762793)
XLA Ops:
  0.0 0.0 copy-start.5
  0.0 0.7 copy-done.5
  0.7 0.0 copy-start
  0.7 1.0 %copy-done = bf16[256,1024]{1,0:T(8,128)(2,1)S(1)} copy-done((bf16[256,1024]{1,0:T(8,128)(2,1)S(1)}, bf16[256,1024]{1,0:T(8,128)(2,1)}, u32[]{:S(2)}) %copy-start) | copy-done | bytes 524312
  1.7 0.0 copy-start.1
  1.7 1.0 %copy-done.1 = bf16[1024,256]{1,0:T(8,128)(2,1)S(1)} copy-done((bf16[1024,256]{1,0:T(8,128)(2,1)S(1)}, bf16[1024,256]{1,0:T(8,128)(2,1)}, u32[]{:S(2)}) %copy-start.1) | copy-done | bytes 524312
  2.8 0.0 copy-start.2
  2.8 1.0 %copy-done.2 = bf16[1024,256]{1,0:T(8,128)(2,1)S(1)} copy-done((bf16[1024,256]{1,0:T(8,128)(2,1)S(1)}, bf16[1024,256]{1,0:T(8,128)(2,1)}, u32[]{:S(2)}) %copy-start.2) | copy-done | bytes 524312
  3.8 0.0 copy-start.3
  3.8 1.0 %copy-done.3 = bf16[1024,256]{1,0:T(8,128)(2,1)S(1)} copy-done((bf16[1024,256]{1,0:T(8,128)(2,1)S(1)}, bf16[1024,256]{1,0:T(8,128)(2,1)}, u32[]{:S(2)}) %copy-start.3) | copy-done | bytes 524312
  4.8 0.0 copy-start.4
  4.9 1.0 %copy-done.4 = bf16[256,1024]{1,0:T(8,128)(2,1)S(1)} copy-done((bf16[256,1024]{1,0:T(8,128)(2,1)S(1)}, bf16[256,1024]{1,0:T(8,128)(2,1)}, u32[]{:S(2)}) %copy-start.4) | copy-done | bytes 524312
  5.9 0.0 copy-start.6
  5.9 0.7 copy-done.6
  6.6 73.7 %layer.1 = bf16[64,1024]{1,0:T(8,128)(2,1)S(1)} custom-call(bf16[256,1024]{1,0:T(8,128)(2,1)S(1)} %copy-done, bf16[1024,256]{1,0:T(8,128)(2,1)S(1)} %copy-done.1, bf16[1024,256]{1,0:T(8,128)(2,1)S(1)} %copy-done.2, bf16[1024,256]{1,0:T(8,128)(2,1)S(1)} %copy-done.3, bf16[256,1024]{1,0:T(8,128)(2,1)S(1)} %copy-done.4, s32[2,3]{1,0:T(2,128)S(1)} %copy-done.5, ...), custom_call_target="tpu_custom_call" | custom-call | tf_op jit(solution)/shard_map/layer/pallas_call | solution.py:370
  80.3 0.7 copy.9
Async XLA Ops:
  0.0 0.7 copy-start.5
  0.7 1.0 %copy-start = (bf16[256,1024]{1,0:T(8,128)(2,1)S(1)}, bf16[256,1024]{1,0:T(8,128)(2,1)}, u32[]{:S(2)}) copy-start(bf16[256,1024]{1,0:T(8,128)(2,1)} %tok_h.1) | copy-start | bytes 1572868
  1.7 1.0 %copy-start.1 = (bf16[1024,256]{1,0:T(8,128)(2,1)S(1)}, bf16[1024,256]{1,0:T(8,128)(2,1)}, u32[]{:S(2)}) copy-start(bf16[1024,256]{1,0:T(8,128)(2,1)} %wq_h.1) | copy-start | bytes 1572868
  2.8 1.0 %copy-start.2 = (bf16[1024,256]{1,0:T(8,128)(2,1)S(1)}, bf16[1024,256]{1,0:T(8,128)(2,1)}, u32[]{:S(2)}) copy-start(bf16[1024,256]{1,0:T(8,128)(2,1)} %wk_h.1) | copy-start | bytes 1572868
  3.8 1.0 %copy-start.3 = (bf16[1024,256]{1,0:T(8,128)(2,1)S(1)}, bf16[1024,256]{1,0:T(8,128)(2,1)}, u32[]{:S(2)}) copy-start(bf16[1024,256]{1,0:T(8,128)(2,1)} %wv_h.1) | copy-start | bytes 1572868
  4.8 1.0 %copy-start.4 = (bf16[256,1024]{1,0:T(8,128)(2,1)S(1)}, bf16[256,1024]{1,0:T(8,128)(2,1)}, u32[]{:S(2)}) copy-start(bf16[256,1024]{1,0:T(8,128)(2,1)} %ow_h.1) | copy-start | bytes 1572868
  5.9 0.7 copy-start.6

commit v2 on v1

v2 whole, which is shorter than its diff:
```python
import functools
import math

import jax
import jax.numpy as jnp
from jax import lax
from jax.experimental import pallas as pl
from jax.experimental.pallas import tpu as pltpu
from jax.sharding import PartitionSpec as P

HEAD_DIM = 64
BLOCK = 128
GLOBALS = 256
RAND = 3
SPREAD = 2
TOK = 256
FEATS = 256
HEADS_HERE = FEATS // HEAD_DIM
LOG2_SCALE = math.log2(math.e) / math.sqrt(HEAD_DIM)
NEG = -1e30
VMEM_LIMIT = 67043328
MESH = pl.DeviceIdType.MESH
F32 = jnp.float32
BF16 = jnp.bfloat16


def dot_nn(a, b):
    return jnp.dot(a, b, preferred_element_type=F32)


def dot_nt(a, b):
    return lax.dot_general(a, b, (((1,), (1,)), ((), ())), preferred_element_type=F32)


def split_of(shards):
    return {128: (4, 4, 4), 32: (4, 2, 2)}[shards]


def scratch_of(split, heads, d):
    y_n, zn_n, zf_n = split
    r = 2 * y_n
    ch = GLOBALS // r
    qc = GLOBALS // y_n
    piece = 2 * FEATS // zn_n
    vm = pltpu.VMEM
    out = {
        "tok": vm((TOK, d), BF16),
        "wq": vm((d, FEATS), BF16),
        "wk": vm((d, FEATS), BF16),
        "wv": vm((d, FEATS), BF16),
        "osl": vm((heads, FEATS, d), BF16),
        "asl": vm((heads - 1, TOK // heads, FEATS), BF16),
        "att": vm((TOK, FEATS), BF16),
        "attl": vm((TOK, FEATS), F32),
        "att_t": vm((FEATS, TOK), F32),
        "q": vm((TOK, FEATS), BF16),
        "kx": vm((10, BLOCK, FEATS), BF16),
        "vx": vm((10, FEATS, BLOCK), BF16),
        "gvt": vm((2, FEATS, BLOCK), BF16),
        "s": vm((7, BLOCK, 2 * BLOCK), F32),
        "peak": vm((4, 1, 2 * BLOCK), F32),
        "total": vm((4, 1, 2 * BLOCK), F32),
        "acc": vm((4, 2 * HEAD_DIM, 2 * BLOCK), F32),
        "pick": vm((TOK, GLOBALS), BF16),
        "kg": vm((r, 2, BLOCK, 2 * HEAD_DIM), BF16),
        "vg": vm((r, 2, 2 * HEAD_DIM, BLOCK), BF16),
        "s2": vm((r, 2 * BLOCK, 2 * qc), F32),
        "q_part": vm((GLOBALS, FEATS), BF16),
        "q_a": vm((r - 1, qc, 2 * HEAD_DIM), BF16),
        "q_bs": vm((qc, 2 * HEAD_DIM), BF16),
        "q_b": vm((zn_n - 1, qc, 2 * HEAD_DIM), BF16),
        "q_cs": vm((qc, 2 * HEAD_DIM), BF16),
        "q_c": vm((zf_n - 1, qc, 2 * HEAD_DIM), BF16),
        "kv_part": vm((GLOBALS, 2 * FEATS), BF16),
        "kv_a": vm((r - 1, ch, 2 * FEATS), BF16),
        "kv_bs": vm((ch, 2 * FEATS), BF16),
        "kv_b": vm((zn_n - 1, ch, piece), BF16),
        "kv_cs": vm((ch, piece), BF16),
        "kv_c": vm((zf_n - 1, ch, piece), BF16),
        "kv_full": vm((GLOBALS, 2 * FEATS), BF16),
        "o_bs": vm((HEAD_DIM, 2 * qc), BF16),
        "o_b": vm((zn_n - 1, HEAD_DIM, 2 * qc), BF16),
        "o_cs": vm((HEAD_DIM, 2 * qc), BF16),
        "o_c": vm((zf_n - 1, HEAD_DIM, 2 * qc), BF16),
        "o_full": vm((GLOBALS, FEATS), BF16),
        "l_bs": vm((1, 2 * qc), F32),
        "l_b": vm((zn_n - 1, 1, 2 * qc), F32),
        "l_cs": vm((1, 2 * qc), F32),
        "l_c": vm((zf_n - 1, 1, 2 * qc), F32),
        "grow": vm((1, GLOBALS), jnp.int32),
        "rand": pltpu.SMEM((2, RAND), jnp.int32),
    }
    z_copies = zn_n + zf_n - 2
    copies = 3 * (r - 1) + 4 * z_copies + (r - 1) + (zn_n - 1) + 12 + 8 + 2 * (heads - 1)
    out["send"] = pltpu.SemaphoreType.DMA((copies,))
    out["recv"] = pltpu.SemaphoreType.DMA((copies,))
    out["load"] = pltpu.SemaphoreType.DMA((7,))
    return out


def kernel(split, heads, names, tok_h, wq_h, wk_h, wv_h, ow_h, rand_h, grow_h, out_v, *scratch):
    m = dict(zip(names, scratch))
    y_n, zn_n, zf_n = split
    r = 2 * y_n
    ch = GLOBALS // r
    qc = GLOBALS // y_n
    piece = 2 * FEATS // zn_n
    half = 2 * HEAD_DIM
    shards = r * zn_n * zf_n
    z_n = zn_n * zf_n
    tm = lax.axis_index("tm")
    hd = lax.axis_index("head")

    order = (("grow", grow_h), ("tok", tok_h), ("wq", wq_h), ("wk", wk_h), ("wv", wv_h))
    order += (("osl", ow_h), ("rand", rand_h))
    loads = {}
    for i, (name, src) in enumerate(order):
        dst = m[name].at[0] if name == "osl" else m[name]
        loads[name] = pltpu.make_async_copy(src, dst, m["load"].at[i])
        loads[name].start()

    y = tm // (2 * z_n)
    z = (tm // 2) % z_n
    c = tm % 2
    j = y * 2 + c
    zn = z % zn_n
    zf = z // zn_n

    def dev_yc(yy, cc):
        return (yy * (2 * z_n) + z * 2 + cc, hd)

    def dev_z(zz):
        return (y * (2 * z_n) + zz * 2 + c, hd)

    steps_j = [(2, 0), (2, 1), (1, 0), (1, 1), (3, 0), (3, 1), (0, 1)]
    there = [((y + dy) % y_n, (c + e) % 2) for dy, e in steps_j]
    group_j = [dev_yc(*at) for at in there]
    near = [(zn + d) % zn_n for d in range(1, zn_n)]
    group_n = [dev_z(zf * zn_n + at) for at in near]
    far_steps = sorted(range(1, zf_n), key=lambda d: -min(d, zf_n - d))
    group_f = [dev_z(((zf + d) % zf_n) * zn_n + zn) for d in far_steps]
    group_h = [(tm, (hd + d) % heads) for d in range(1, heads)]
    steps_w = (2, -2, 1, -1)
    group_w = [((tm + d + shards) % shards, hd) for d in steps_w]
    everyone = group_j + group_n + group_f + group_h + group_w

    barrier = pltpu.get_barrier_semaphore()
    for dev in everyone:
        pl.semaphore_signal(barrier, inc=1, device_id=dev, device_id_type=MESH)

    count = [0]
    started = []

    def send(src, dst, dev):
        n = count[0]
        count[0] += 1
        copy = pltpu.make_async_remote_copy(
            src_ref=src,
            dst_ref=dst,
            send_sem=m["send"].at[n],
            recv_sem=m["recv"].at[n],
            device_id=dev,
            device_id_type=MESH,
        )
        copy.start()
        started.append(copy)
        return copy

    def part_of(at, size):
        return pl.ds(pl.multiple_of(at * size, size), size)

    def gather(first, copies, slots):
        total = first.astype(F32)
        for n, copy in enumerate(copies):
            copy.wait_recv()
            total = total + slots[n].astype(F32)
        return total.astype(BF16)

    def to_all(src, dst, group):
        return [send(src, dst.at[n], dev) for n, dev in enumerate(group)]

    loads["grow"].wait()
    spots = lax.broadcasted_iota(jnp.int32, (TOK, GLOBALS), 0) + tm * TOK
    pick = jnp.where(spots == m["grow"][...], 1.0, 0.0).astype(F32)
    m["pick"][...] = pick.astype(BF16)
    pick_t = pick.T.astype(BF16)
    loads["tok"].wait()
    loads["wq"].wait()
    q = dot_nn(m["tok"][...], m["wq"][...]).astype(BF16)
    m["q"][...] = q
    m["q_part"][...] = dot_nn(pick_t, q).astype(BF16)
    pl.semaphore_wait(barrier, len(everyone))
    qa = [
        send(m["q_part"].at[part_of(yy, qc), part_of(cc, half)], m["q_a"].at[n], group_j[n])
        for n, (yy, cc) in enumerate(there)
    ]

    loads["wk"].wait()
    k = dot_nn(m["tok"][...], m["wk"][...]).astype(BF16)
    m["kv_part"][:, :FEATS] = dot_nn(pick_t, k).astype(BF16)
    for b in range(2):
        m["kx"][4 + b] = k[b * BLOCK : (b + 1) * BLOCK]
    loads["wv"].wait()
    v32 = dot_nn(m["tok"][...], m["wv"][...])
    m["kv_part"][:, FEATS:] = dot_nn(pick_t, v32.astype(BF16)).astype(BF16)
    kva = [
        send(m["kv_part"].at[part_of(yy * 2 + cc, ch)], m["kv_a"].at[n], group_j[n])
        for n, (yy, cc) in enumerate(there)
    ]
    v_t = v32.T.astype(BF16)
    for b in range(2):
        m["vx"][4 + b] = v_t[:, b * BLOCK : (b + 1) * BLOCK]

    kg_in, vg_in = {}, {}
    for (dy, e), (yy, cc), dev in zip(steps_j, there, group_j):
        if dy == 2:
            continue
        slot = ((y_n - dy) % y_n) * 2 + e
        kg_in[(dy, e)] = send(m["kx"].at[pl.ds(4, 2), :, part_of(cc, half)], m["kg"].at[slot], dev)
        vg_in[(dy, e)] = send(m["vx"].at[pl.ds(4, 2), part_of(cc, half), :], m["vg"].at[slot], dev)

    def start_window(name):
        return [
            send(m[name].at[pl.ds(4, 2)], m[name].at[pl.ds(2 * (SPREAD - step), 2)], dev)
            for step, dev in zip(steps_w, group_w)
        ]

    window = start_window("kx")
    loads["osl"].wait()
    ow = [send(m["osl"].at[0], m["osl"].at[d + 1], group_h[d]) for d in range(heads - 1)]
    for b in range(2):
        m["kg"][0, b] = m["kx"][4 + b, :, part_of(c, half)]
        m["vg"][0, b] = m["vx"][4 + b, part_of(c, half), :]

    m["q_bs"][...] = gather(m["q_part"][part_of(y, qc), part_of(c, half)], qa, m["q_a"])
    qb = to_all(m["q_bs"], m["q_b"], group_n)
    m["kv_bs"][...] = gather(m["kv_part"][part_of(j, ch), :], kva, m["kv_a"])
    kvb = [
        send(m["kv_bs"].at[:, part_of(at, piece)], m["kv_b"].at[n], group_n[n])
        for n, at in enumerate(near)
    ]
    m["q_cs"][...] = gather(m["q_bs"][...], qb, m["q_b"])
    qcs = to_all(m["q_cs"], m["q_c"], group_f)
    m["kv_cs"][...] = gather(m["kv_bs"][:, part_of(zn, piece)], kvb, m["kv_b"])
    kvc = to_all(m["kv_cs"], m["kv_c"], group_f)
    window += start_window("vx")

    for e in range(2):
        kg_in.pop((1, e)).wait_recv()
    forward = [send(m["kg"].at[pl.ds(6, 2)], m["kg"].at[pl.ds(4, 2)], group_j[2])]
    for e in range(2):
        vg_in.pop((3, e)).wait_recv()
    forward += [send(m["vg"].at[pl.ds(2, 2)], m["vg"].at[pl.ds(4, 2)], group_j[4])]

    gq = gather(m["q_cs"][...], qcs, m["q_c"])
    for copy in list(kg_in.values()) + list(vg_in.values()) + forward:
        copy.wait_recv()

    def head_mask(h, width):
        lane_head = lax.broadcasted_iota(jnp.int32, (1, width), 1) // HEAD_DIM
        return jnp.where(lane_head == h, 1.0, 0.0).astype(BF16)

    gq2 = jnp.concatenate([gq * head_mask(0, half), gq * head_mask(1, half)], axis=0)
    peak = None
    for n in range(r):
        s = dot_nt(m["kg"][n].reshape(2 * BLOCK, half), gq2) * LOG2_SCALE
        m["s2"][n] = s
        top = jnp.max(s, axis=0, keepdims=True)
        peak = top if peak is None else jnp.maximum(peak, top)
    total = jnp.zeros((1, 2 * qc), F32)
    acc = jnp.zeros((half, 2 * qc), F32)
    for n in range(r):
        e = jnp.exp2(m["s2"][n] - peak)
        total = total + jnp.sum(e, axis=0, keepdims=True)
        e = e.astype(BF16)
        acc = acc + dot_nn(m["vg"][n, 0], e[:BLOCK]) + dot_nn(m["vg"][n, 1], e[BLOCK:])
    first = lax.broadcasted_iota(jnp.int32, (1, 2 * qc), 1) < qc
    acc = jnp.where(first, acc[:HEAD_DIM], acc[HEAD_DIM:])
    m["o_bs"][...] = (acc / total).astype(BF16)
    m["l_bs"][...] = peak + jnp.log2(total)

    def combine(tag, copies):
        for copy in copies:
            copy.wait_recv()
        slots = "b" if tag == "bs" else "c"
        size = len(copies) // 2
        logs = [m["l_" + tag][...]] + [m["l_" + slots][n] for n in range(size)]
        peak = functools.reduce(jnp.maximum, logs)
        shares = [jnp.exp2(x - peak) for x in logs]
        total = functools.reduce(jnp.add, shares)
        acc = m["o_" + tag][...].astype(F32) * shares[0]
        for n in range(size):
            acc = acc + m["o_" + slots][n].astype(F32) * shares[n + 1]
        return acc / total, peak + jnp.log2(total)

    ob = to_all(m["o_bs"], m["o_b"], group_n) + to_all(m["l_bs"], m["l_b"], group_n)

    mine = m["kv_full"].at[part_of(j, ch), part_of(zn, piece)]
    m["kv_full"][part_of(j, ch), part_of(zn, piece)] = gather(m["kv_cs"][...], kvc, m["kv_c"])
    kve = [send(mine, mine, dev) for dev in group_n]

    o, l = combine("bs", ob)
    m["o_cs"][...] = o.astype(BF16)
    m["l_cs"][...] = l
    oc = to_all(m["o_cs"], m["o_c"], group_f) + to_all(m["l_cs"], m["l_c"], group_f)

    for copy in kve:
        copy.wait_recv()
    mine = m["kv_full"].at[part_of(j, ch), :]
    kvd = [send(mine, mine, dev) for dev in group_j]

    loads["rand"].wait()
    for copy in window:
        copy.wait_recv()
    blocks = 2 * shards

    def queries_of(jb, pair):
        qb_here = m["q"][part_of(jb, BLOCK), :]
        return jnp.concatenate(
            [qb_here * head_mask(2 * pair, FEATS), qb_here * head_mask(2 * pair + 1, FEATS)],
            axis=0,
        )

    def attend_near(step, carry):
        jb = step // 2
        pair = step % 2
        q2 = queries_of(jb, pair)
        feats = part_of(pair, half)
        spots_x = [2 + jb + w for w in range(4)]
        spots_x += [
            jnp.clip(m["rand"][jb, n] - 2 * tm + 2 * SPREAD, 0, 9) for n in range(RAND)
        ]
        peak = None
        for n in range(7):
            s = dot_nt(m["kx"][spots_x[n]], q2) * LOG2_SCALE
            if n in (0, 1, 3):
                block = 2 * tm + jb + n - 2
                inside = (block >= 0) & (block < blocks)
                s = jnp.where(inside, s, NEG)
            m["s"][n] = s
            top = jnp.max(s, axis=0, keepdims=True)
            peak = top if peak is None else jnp.maximum(peak, top)
        total = jnp.zeros((1, 2 * BLOCK), F32)
        acc = jnp.zeros((half, 2 * BLOCK), F32)
        for n in range(7):
            e = jnp.exp2(m["s"][n] - peak)
            total = total + jnp.sum(e, axis=0, keepdims=True)
            acc = acc + dot_nn(m["vx"][spots_x[n], feats, :], e.astype(BF16))
        m["peak"][step] = peak
        m["total"][step] = total
        m["acc"][step] = acc
        return carry

    lax.fori_loop(0, 4, attend_near, 0)

    for copy in kvd:
        copy.wait_recv()
    gv_t = m["kv_full"][:, FEATS:].astype(F32).T.astype(BF16)
    for b in range(2):
        m["gvt"][b] = gv_t[:, b * BLOCK : (b + 1) * BLOCK]

    def attend_global(step, carry):
        jb = step // 2
        pair = step % 2
        q2 = queries_of(jb, pair)
        feats = part_of(pair, half)
        s = dot_nt(m["kv_full"][:, :FEATS], q2) * LOG2_SCALE
        before = m["peak"][step]
        peak = jnp.maximum(before, jnp.max(s, axis=0, keepdims=True))
        e = jnp.exp2(s - peak)
        share = jnp.exp2(before - peak)
        total = m["total"][step] * share + jnp.sum(e, axis=0, keepdims=True)
        e = e.astype(BF16)
        acc = m["acc"][step] * share
        for b in range(2):
            acc = acc + dot_nn(m["gvt"][b, feats, :], e[b * BLOCK : (b + 1) * BLOCK])
        acc = acc / total
        for n in range(2):
            m["att_t"][part_of(pair * 2 + n, HEAD_DIM), part_of(jb, BLOCK)] = acc[
                n * HEAD_DIM : (n + 1) * HEAD_DIM, n * BLOCK : (n + 1) * BLOCK
            ]
        return carry

    lax.fori_loop(0, 4, attend_global, 0)
    is_global = jnp.max(m["pick"][...].astype(F32), axis=1, keepdims=True)
    m["attl"][...] = jnp.where(is_global > 0.5, 0.0, m["att_t"][...].T)

    o, _ = combine("cs", oc)
    o_t = o.T
    o_t = jnp.concatenate([o_t[:qc], o_t[qc:]], axis=1).astype(BF16)
    m["o_full"][part_of(y, qc), part_of(c, half)] = o_t
    mine = m["o_full"].at[part_of(y, qc), part_of(c, half)]
    od = [send(mine, mine, dev) for dev in group_j]
    for copy in od:
        copy.wait_recv()

    placed = dot_nn(m["pick"][...], m["o_full"][...])
    m["att"][...] = (placed + m["attl"][...]).astype(BF16)
    per = TOK // heads
    ax = [
        send(m["att"].at[part_of((hd + d + 1) % heads, per)], m["asl"].at[d], group_h[d])
        for d in range(heads - 1)
    ]
    mixed = dot_nn(m["att"][part_of(hd, per)], m["osl"][0])
    for d in range(heads - 1):
        ow[d].wait_recv()
        ax[d].wait_recv()
        mixed = mixed + dot_nn(m["asl"][d], m["osl"][d + 1])
    out_v[...] = mixed.astype(BF16)
    for copy in started:
        copy.wait_send()


def shards_fn(tokens, q_weight, k_weight, v_weight, o_weight, rand_blocks, global_pos):
    shards = lax.axis_size("tm")
    heads = lax.axis_size("head")
    split = split_of(shards)
    d = tokens.shape[1]
    scratch = scratch_of(split, heads, d)
    hbm = pl.BlockSpec(memory_space=pl.ANY)
    return pl.pallas_call(
        functools.partial(kernel, split, heads, list(scratch)),
        out_shape=jax.ShapeDtypeStruct((TOK // heads, d), BF16),
        in_specs=[hbm] * 7,
        out_specs=pl.BlockSpec(memory_space=pltpu.VMEM),
        scratch_shapes=list(scratch.values()),
        compiler_params=pltpu.CompilerParams(
            collective_id=0, has_side_effects=True, vmem_limit_bytes=VMEM_LIMIT
        ),
        name="layer",
    )(
        tokens,
        q_weight,
        k_weight,
        v_weight,
        o_weight,
        rand_blocks,
        global_pos.reshape(1, GLOBALS),
    )


def solution(mesh):
    placed = (
        P("tm", None),
        P(None, "head"),
        P(None, "head"),
        P(None, "head"),
        P("head", None),
        P("tm", None),
        P(),
    )
    return jax.shard_map(
        shards_fn, mesh=mesh, in_specs=placed, out_specs=P(("tm", "head"), None), check_vma=False
    )
```

time: 81.3 us -> 63.8 us (0.78)
  Pallas kernels: 73.7 us -> 61.6 us
  local copies, waits for them, and re-layouts: 7.22 us -> 1.57 us
    pallas_call x1, Pallas kernels: 73.7 us -> 61.6 us  [shards_fn(): pl.pallas_call(functools.partial(kernel, split, heads, list(scratch)), ou...]
    unnamed x15 -> x1, local copies, waits for them, and re-layouts: 7.22 us -> 1.57 us
where the time goes in v2:
time: 63.8 us; the launch traced here: 63.2 us
  Pallas kernels  61.6 us (97%)
  local copies, waits for them, and re-layouts  1.57 us (2%)
    pallas_call x1, Pallas kernels, shards_fn(): pl.pallas_call(functools.partial(kernel, split, heads, list(scratch)), ou...  61.6 us
    unnamed x1, local copies, waits for them, and re-layouts  1.57 us

profile of v2, /device:TPU:1, one launch (start us, length us, event | category | flops | bytes accessed | tf_op | source)
XLA Modules:
  0.0 63.2 jit_solution(15249454476740747437)
XLA Ops:
  0.0 61.6 %layer.1 = bf16[64,1024]{1,0:T(8,128)(2,1)} custom-call(bf16[256,1024]{1,0:T(8,128)(2,1)} %tok_h.1, bf16[1024,256]{1,0:T(8,128)(2,1)} %wq_h.1, bf16[1024,256]{1,0:T(8,128)(2,1)} %wk_h.1, bf16[1024,256]{1,0:T(8,128)(2,1)} %wv_h.1, bf16[256,1024]{1,0:T(8,128)(2,1)} %ow_h.1, s32[2,3]{1,0:T(2,128)} %rand_h.1, s32[1,256]{1,0:T(1,128)} %bitcast.1), custom_call_target="tpu_custom_call" | custom-call | tf_op jit(solution)/shard_map/layer/pallas_call | solution.py:421
  61.6 1.6 %copy.9 = bf16[64,1024]{1,0:T(8,128)(2,1)} copy(bf16[64,1024]{1,0:T(8,128)(2,1)} %layer.1) | data formatting | bytes 262144

commit v3 on v2

--- a/solution.py
+++ b/solution.py
@@ -18,7 +18,7 @@
 HEADS_HERE = FEATS // HEAD_DIM
 LOG2_SCALE = math.log2(math.e) / math.sqrt(HEAD_DIM)
 NEG = -1e30
-VMEM_LIMIT = 67043328
+VMEM_LIMIT = 56000000
 MESH = pl.DeviceIdType.MESH
 F32 = jnp.float32
 BF16 = jnp.bfloat16
@@ -91,9 +91,10 @@
         "rand": pltpu.SMEM((2, RAND), jnp.int32),
     }
     z_copies = zn_n + zf_n - 2
-    copies = 3 * (r - 1) + 4 * z_copies + (r - 1) + (zn_n - 1) + 12 + 8 + 2 * (heads - 1)
+    copies = 3 * (r - 1) + 4 * z_copies + (r - 1) + (zn_n - 1) + 2 * (r - 2) + 8 + 2 * (heads - 1)
     out["send"] = pltpu.SemaphoreType.DMA((copies,))
     out["recv"] = pltpu.SemaphoreType.DMA((copies,))
+    out["greet"] = pltpu.SemaphoreType.REGULAR
     out["load"] = pltpu.SemaphoreType.DMA((7,))
     return out
 
@@ -140,9 +141,12 @@
     far_steps = sorted(range(1, zf_n), key=lambda d: -min(d, zf_n - d))
     group_f = [dev_z(((zf + d) % zf_n) * zn_n + zn) for d in far_steps]
     group_h = [(tm, (hd + d) % heads) for d in range(1, heads)]
-    steps_w = (2, -2, 1, -1)
+    steps_w = (2, -2)
+    partner = dev_yc(y, 1 - c)
     group_w = [((tm + d + shards) % shards, hd) for d in steps_w]
-    everyone = group_j + group_n + group_f + group_h + group_w
+    next_f = [dev for d, dev in zip(far_steps, group_f) if min(d, zf_n - d) == 1]
+    relayed = len(next_f) < len(group_f)
+    everyone = group_j + group_n + next_f + group_h + group_w
 
     barrier = pltpu.get_barrier_semaphore()
     for dev in everyone:
@@ -151,7 +155,7 @@
     count = [0]
     started = []
 
-    def send(src, dst, dev):
+    def plan(src, dst, dev):
         n = count[0]
         count[0] += 1
         copy = pltpu.make_async_remote_copy(
@@ -162,8 +166,12 @@
             device_id=dev,
             device_id_type=MESH,
         )
+        started.append(copy)
+        return copy
+
+    def send(src, dst, dev):
+        copy = plan(src, dst, dev)
         copy.start()
-        started.append(copy)
         return copy
 
     def part_of(at, size):
@@ -190,6 +198,9 @@
     m["q"][...] = q
     m["q_part"][...] = dot_nn(pick_t, q).astype(BF16)
     pl.semaphore_wait(barrier, len(everyone))
+    if relayed:
+        for dev in next_f:
+            pl.semaphore_signal(m["greet"], inc=1, device_id=dev, device_id_type=MESH)
     qa = [
         send(m["q_part"].at[part_of(yy, qc), part_of(cc, half)], m["q_a"].at[n], group_j[n])
         for n, (yy, cc) in enumerate(there)
@@ -211,48 +222,62 @@
     for b in range(2):
         m["vx"][4 + b] = v_t[:, b * BLOCK : (b + 1) * BLOCK]
 
+
+    edges = (z == z_n - 1, z == 0)
+    window, beside = [], []
+    for name in ("kx", "vx"):
+        own = m[name].at[pl.ds(4, 2)]
+        for step, dev in zip(steps_w, group_w):
+            window.append(plan(own, m[name].at[pl.ds(2 * (SPREAD - step), 2)], dev))
+        beside.append(send(own, m[name].at[pl.ds(2 + 4 * c, 2)], partner))
+
+    def start_window(copies, at_edge):
+        for n, copy in enumerate(copies):
+            pl.when(edges[n % 2] if at_edge else jnp.logical_not(edges[n % 2]))(copy.start)
+
+    start_window(window[:2], False)
+    loads["osl"].wait()
+    ow = [send(m["osl"].at[0], m["osl"].at[d + 1], group_h[d]) for d in range(heads - 1)]
+    for b in range(2):
+        m["kg"][0, b] = m["kx"][4 + b, :, part_of(c, half)]
+        m["vg"][0, b] = m["vx"][4 + b, part_of(c, half), :]
+
+    m["q_bs"][...] = gather(m["q_part"][part_of(y, qc), part_of(c, half)], qa, m["q_a"])
+    qb = to_all(m["q_bs"], m["q_b"], group_n)
     kg_in, vg_in = {}, {}
     for (dy, e), (yy, cc), dev in zip(steps_j, there, group_j):
         if dy == 2:
             continue
         slot = ((y_n - dy) % y_n) * 2 + e
-        kg_in[(dy, e)] = send(m["kx"].at[pl.ds(4, 2), :, part_of(cc, half)], m["kg"].at[slot], dev)
-        vg_in[(dy, e)] = send(m["vx"].at[pl.ds(4, 2), part_of(cc, half), :], m["vg"].at[slot], dev)
-
-    def start_window(name):
-        return [
-            send(m[name].at[pl.ds(4, 2)], m[name].at[pl.ds(2 * (SPREAD - step), 2)], dev)
-            for step, dev in zip(steps_w, group_w)
-        ]
-
-    window = start_window("kx")
-    loads["osl"].wait()
-    ow = [send(m["osl"].at[0], m["osl"].at[d + 1], group_h[d]) for d in range(heads - 1)]
-    for b in range(2):
-        m["kg"][0, b] = m["kx"][4 + b, :, part_of(c, half)]
-        m["vg"][0, b] = m["vx"][4 + b, part_of(c, half), :]
-
-    m["q_bs"][...] = gather(m["q_part"][part_of(y, qc), part_of(c, half)], qa, m["q_a"])
-    qb = to_all(m["q_bs"], m["q_b"], group_n)
+        ks = m["kx"].at[pl.ds(4, 2), :, part_of(cc, half)]
+        vs = m["vx"].at[pl.ds(4, 2), part_of(cc, half), :]
+        ways = [(kg_in, ks, "kg"), (vg_in, vs, "vg")]
+        for way, src, name in ways if dy == 1 else ways[::-1]:
+            way[(dy, e)] = send(src, m[name].at[slot], dev)
     m["kv_bs"][...] = gather(m["kv_part"][part_of(j, ch), :], kva, m["kv_a"])
     kvb = [
         send(m["kv_bs"].at[:, part_of(at, piece)], m["kv_b"].at[n], group_n[n])
         for n, at in enumerate(near)
     ]
     m["q_cs"][...] = gather(m["q_bs"][...], qb, m["q_b"])
+    if relayed:
+        pl.semaphore_wait(m["greet"], len(next_f))
     qcs = to_all(m["q_cs"], m["q_c"], group_f)
     m["kv_cs"][...] = gather(m["kv_bs"][:, part_of(zn, piece)], kvb, m["kv_b"])
     kvc = to_all(m["kv_cs"], m["kv_c"], group_f)
-    window += start_window("vx")
-
+    start_window(window[2:], False)
     for e in range(2):
         kg_in.pop((1, e)).wait_recv()
     forward = [send(m["kg"].at[pl.ds(6, 2)], m["kg"].at[pl.ds(4, 2)], group_j[2])]
     for e in range(2):
         vg_in.pop((3, e)).wait_recv()
     forward += [send(m["vg"].at[pl.ds(2, 2)], m["vg"].at[pl.ds(4, 2)], group_j[4])]
-
     gq = gather(m["q_cs"][...], qcs, m["q_c"])
+    start_window(window, True)
+    mine = m["kv_full"].at[part_of(j, ch), part_of(zn, piece)]
+    m["kv_full"][part_of(j, ch), part_of(zn, piece)] = gather(m["kv_cs"][...], kvc, m["kv_c"])
+    kve = [send(mine, mine, dev) for dev in group_n]
+
     for copy in list(kg_in.values()) + list(vg_in.values()) + forward:
         copy.wait_recv()
 
@@ -295,22 +320,24 @@
 
     ob = to_all(m["o_bs"], m["o_b"], group_n) + to_all(m["l_bs"], m["l_b"], group_n)
 
-    mine = m["kv_full"].at[part_of(j, ch), part_of(zn, piece)]
-    m["kv_full"][part_of(j, ch), part_of(zn, piece)] = gather(m["kv_cs"][...], kvc, m["kv_c"])
-    kve = [send(mine, mine, dev) for dev in group_n]
+    for copy in kve:
+        copy.wait_recv()
+    mine = m["kv_full"].at[part_of(j, ch), :]
+    kvd = [send(mine, mine, dev) for dev in group_j]
 
     o, l = combine("bs", ob)
     m["o_cs"][...] = o.astype(BF16)
     m["l_cs"][...] = l
     oc = to_all(m["o_cs"], m["o_c"], group_f) + to_all(m["l_cs"], m["l_c"], group_f)
 
-    for copy in kve:
-        copy.wait_recv()
-    mine = m["kv_full"].at[part_of(j, ch), :]
-    kvd = [send(mine, mine, dev) for dev in group_j]
-
+    for copy in window:
+        copy.wait_recv()
+    for name in ("kx", "vx"):
+        beside.append(
+            send(m[name].at[pl.ds(8 - 8 * c, 2)], m[name].at[pl.ds(6 - 4 * c, 2)], partner)
+        )
     loads["rand"].wait()
-    for copy in window:
+    for copy in beside:
         copy.wait_recv()
     blocks = 2 * shards
 
@@ -351,7 +378,8 @@
         m["acc"][step] = acc
         return carry
 
-    lax.fori_loop(0, 4, attend_near, 0)
+    for step in range(4):
+        attend_near(step, 0)
 
     for copy in kvd:
         copy.wait_recv()
@@ -381,7 +409,8 @@
             ]
         return carry
 
-    lax.fori_loop(0, 4, attend_global, 0)
+    for step in range(4):
+        attend_global(step, 0)
     is_global = jnp.max(m["pick"][...].astype(F32), axis=1, keepdims=True)
     m["attl"][...] = jnp.where(is_global > 0.5, 0.0, m["att_t"][...].T)
 

time: 63.8 us -> 58.3 us (0.914)
  Pallas kernels: 61.6 us -> 56.1 us
    pallas_call x1, Pallas kernels: 61.6 us -> 56.1 us  [shards_fn(): pl.pallas_call(functools.partial(kernel, split, heads, list(scratch)), ou...]
    unnamed x1 -> x5, local copies, waits for them, and re-layouts: 1.57 us -> 2.01 us
where the time goes in v3:
time: 58.3 us; the launch traced here: 58.1 us
  Pallas kernels  56.1 us (96%)
  local copies, waits for them, and re-layouts  2.01 us (3%)
    pallas_call x1, Pallas kernels, shards_fn(): pl.pallas_call(functools.partial(kernel, split, heads, list(scratch)), ou...  56.1 us
    unnamed x5, local copies, waits for them, and re-layouts  2.01 us

profile of v3, /device:TPU:1, one launch (start us, length us, event | category | flops | bytes accessed | tf_op | source)
XLA Modules:
  0.0 58.1 jit_solution(918682388037560170)
XLA Ops:
  0.0 0.0 copy-start
  0.0 0.7 %copy-done = s32[2,3]{1,0:T(2,128)S(1)} copy-done((s32[2,3]{1,0:T(2,128)S(1)}, s32[2,3]{1,0:T(2,128)}, u32[]{:S(2)}) %copy-start) | copy-done | bytes 48
  0.7 0.0 copy-start.1
  0.7 0.7 %copy-done.1 = s32[256]{0:T(256)S(1)} copy-done((s32[256]{0:T(256)S(1)}, s32[256]{0:T(256)}, u32[]{:S(2)}) %copy-start.1) | copy-done | bytes 1048
  1.4 56.1 %layer.1 = bf16[64,1024]{1,0:T(8,128)(2,1)S(1)} custom-call(bf16[256,1024]{1,0:T(8,128)(2,1)} %tok_h.1, bf16[1024,256]{1,0:T(8,128)(2,1)} %wq_h.1, bf16[1024,256]{1,0:T(8,128)(2,1)} %wk_h.1, bf16[1024,256]{1,0:T(8,128)(2,1)} %wv_h.1, bf16[256,1024]{1,0:T(8,128)(2,1)} %ow_h.1, s32[2,3]{1,0:T(2,128)S(1)} %copy-done, s32[1,256]{1,0:T(1,128)S(1)} %bitcast.1), custom_call_target="tpu_custom_call" | custom-call | tf_op jit(solution)/shard_map/layer/pallas_call | solution.py:450
  57.5 0.7 %copy.9 = bf16[64,1024]{1,0:T(8,128)(2,1)} copy(bf16[64,1024]{1,0:T(8,128)(2,1)S(1)} %layer.1) | data formatting | bytes 262144
Async XLA Ops:
  0.0 0.7 %copy-start = (s32[2,3]{1,0:T(2,128)S(1)}, s32[2,3]{1,0:T(2,128)}, u32[]{:S(2)}) copy-start(s32[2,3]{1,0:T(2,128)} %rand_h.1) | copy-start | bytes 76
  0.7 0.7 %copy-start.1 = (s32[256]{0:T(256)S(1)}, s32[256]{0:T(256)}, u32[]{:S(2)}) copy-start(s32[256]{0:T(256)} %param.13) | copy-start | bytes 3076

commit v4 on v3

--- a/solution.py
+++ b/solution.py
@@ -34,6 +34,12 @@
 
 def split_of(shards):
     return {128: (4, 4, 4), 32: (4, 2, 2)}[shards]
+
+
+class Group:
+    def __init__(self, going, coming):
+        self.wait_send = going.wait
+        self.wait_recv = coming.wait
 
 
 def scratch_of(split, heads, d):
@@ -90,8 +96,7 @@
         "grow": vm((1, GLOBALS), jnp.int32),
         "rand": pltpu.SMEM((2, RAND), jnp.int32),
     }
-    z_copies = zn_n + zf_n - 2
-    copies = 3 * (r - 1) + 4 * z_copies + (r - 1) + (zn_n - 1) + 2 * (r - 2) + 8 + 2 * (heads - 1)
+    copies = 31
     out["send"] = pltpu.SemaphoreType.DMA((copies,))
     out["recv"] = pltpu.SemaphoreType.DMA((copies,))
     out["greet"] = pltpu.SemaphoreType.REGULAR
@@ -174,18 +179,34 @@
         copy.start()
         return copy
 
+    def send_all(items, like):
+        n = count[0]
+        count[0] += 1
+        for src, dst, dev in items:
+            pltpu.make_async_remote_copy(
+                src_ref=src,
+                dst_ref=dst,
+                send_sem=m["send"].at[n],
+                recv_sem=m["recv"].at[n],
+                device_id=dev,
+                device_id_type=MESH,
+            ).start()
+        group = Group(*(pltpu.make_async_copy(like, like, m[way].at[n]) for way in ("send", "recv")))
+        started.append(group)
+        return group
+
     def part_of(at, size):
         return pl.ds(pl.multiple_of(at * size, size), size)
 
-    def gather(first, copies, slots):
+    def gather(first, group, slots):
+        group.wait_recv()
         total = first.astype(F32)
-        for n, copy in enumerate(copies):
-            copy.wait_recv()
+        for n in range(slots.shape[0]):
             total = total + slots[n].astype(F32)
         return total.astype(BF16)
 
     def to_all(src, dst, group):
-        return [send(src, dst.at[n], dev) for n, dev in enumerate(group)]
+        return send_all([(src, dst.at[n], dev) for n, dev in enumerate(group)], dst)
 
     loads["grow"].wait()
     spots = lax.broadcasted_iota(jnp.int32, (TOK, GLOBALS), 0) + tm * TOK
@@ -201,10 +222,8 @@
     if relayed:
         for dev in next_f:
             pl.semaphore_signal(m["greet"], inc=1, device_id=dev, device_id_type=MESH)
-    qa = [
-        send(m["q_part"].at[part_of(yy, qc), part_of(cc, half)], m["q_a"].at[n], group_j[n])
-        for n, (yy, cc) in enumerate(there)
-    ]
+    pieces = [m["q_part"].at[part_of(yy, qc), part_of(cc, half)] for yy, cc in there]
+    qa = send_all([(src, m["q_a"].at[n], group_j[n]) for n, src in enumerate(pieces)], m["q_a"])
 
     loads["wk"].wait()
     k = dot_nn(m["tok"][...], m["wk"][...]).astype(BF16)
@@ -214,10 +233,8 @@
     loads["wv"].wait()
     v32 = dot_nn(m["tok"][...], m["wv"][...])
     m["kv_part"][:, FEATS:] = dot_nn(pick_t, v32.astype(BF16)).astype(BF16)
-    kva = [
-        send(m["kv_part"].at[part_of(yy * 2 + cc, ch)], m["kv_a"].at[n], group_j[n])
-        for n, (yy, cc) in enumerate(there)
-    ]
+    pieces = [m["kv_part"].at[part_of(yy * 2 + cc, ch)] for yy, cc in there]
+    kva = send_all([(src, m["kv_a"].at[n], group_j[n]) for n, src in enumerate(pieces)], m["kv_a"])
     v_t = v32.T.astype(BF16)
     for b in range(2):
         m["vx"][4 + b] = v_t[:, b * BLOCK : (b + 1) * BLOCK]
@@ -237,28 +254,33 @@
 
     start_window(window[:2], False)
     loads["osl"].wait()
-    ow = [send(m["osl"].at[0], m["osl"].at[d + 1], group_h[d]) for d in range(heads - 1)]
+    ow = send_all(
+        [(m["osl"].at[0], m["osl"].at[d + 1], dev) for d, dev in enumerate(group_h)],
+        m["osl"].at[pl.ds(1, heads - 1)],
+    )
     for b in range(2):
         m["kg"][0, b] = m["kx"][4 + b, :, part_of(c, half)]
         m["vg"][0, b] = m["vx"][4 + b, part_of(c, half), :]
 
     m["q_bs"][...] = gather(m["q_part"][part_of(y, qc), part_of(c, half)], qa, m["q_a"])
     qb = to_all(m["q_bs"], m["q_b"], group_n)
-    kg_in, vg_in = {}, {}
-    for (dy, e), (yy, cc), dev in zip(steps_j, there, group_j):
-        if dy == 2:
-            continue
-        slot = ((y_n - dy) % y_n) * 2 + e
-        ks = m["kx"].at[pl.ds(4, 2), :, part_of(cc, half)]
-        vs = m["vx"].at[pl.ds(4, 2), part_of(cc, half), :]
-        ways = [(kg_in, ks, "kg"), (vg_in, vs, "vg")]
-        for way, src, name in ways if dy == 1 else ways[::-1]:
-            way[(dy, e)] = send(src, m[name].at[slot], dev)
+    kvg = {}
+    for dy in (1, 3, 0):
+        at = [n for n, step in enumerate(steps_j) if step[0] == dy]
+        slots = [((y_n - dy) % y_n) * 2 + steps_j[n][1] for n in at]
+        ways = [(m["kx"].at[pl.ds(4, 2), :, part_of(there[n][1], half)], "kg") for n in at]
+        ways = [ways] + [
+            [(m["vx"].at[pl.ds(4, 2), part_of(there[n][1], half), :], "vg") for n in at]
+        ]
+        for way in ways if dy == 1 else ways[::-1]:
+            name = way[0][1]
+            kvg[(name, dy)] = send_all(
+                [(way[i][0], m[name].at[slots[i]], group_j[n]) for i, n in enumerate(at)],
+                m[name].at[pl.ds(0, len(at))],
+            )
     m["kv_bs"][...] = gather(m["kv_part"][part_of(j, ch), :], kva, m["kv_a"])
-    kvb = [
-        send(m["kv_bs"].at[:, part_of(at, piece)], m["kv_b"].at[n], group_n[n])
-        for n, at in enumerate(near)
-    ]
+    pieces = [m["kv_bs"].at[:, part_of(at, piece)] for at in near]
+    kvb = send_all([(src, m["kv_b"].at[n], group_n[n]) for n, src in enumerate(pieces)], m["kv_b"])
     m["q_cs"][...] = gather(m["q_bs"][...], qb, m["q_b"])
     if relayed:
         pl.semaphore_wait(m["greet"], len(next_f))
@@ -266,19 +288,13 @@
     m["kv_cs"][...] = gather(m["kv_bs"][:, part_of(zn, piece)], kvb, m["kv_b"])
     kvc = to_all(m["kv_cs"], m["kv_c"], group_f)
     start_window(window[2:], False)
-    for e in range(2):
-        kg_in.pop((1, e)).wait_recv()
+    kvg.pop(("kg", 1)).wait_recv()
     forward = [send(m["kg"].at[pl.ds(6, 2)], m["kg"].at[pl.ds(4, 2)], group_j[2])]
-    for e in range(2):
-        vg_in.pop((3, e)).wait_recv()
+    kvg.pop(("vg", 3)).wait_recv()
     forward += [send(m["vg"].at[pl.ds(2, 2)], m["vg"].at[pl.ds(4, 2)], group_j[4])]
     gq = gather(m["q_cs"][...], qcs, m["q_c"])
     start_window(window, True)
-    mine = m["kv_full"].at[part_of(j, ch), part_of(zn, piece)]
-    m["kv_full"][part_of(j, ch), part_of(zn, piece)] = gather(m["kv_cs"][...], kvc, m["kv_c"])
-    kve = [send(mine, mine, dev) for dev in group_n]
-
-    for copy in list(kg_in.values()) + list(vg_in.values()) + forward:
+    for copy in list(kvg.values()) + forward:
         copy.wait_recv()
 
     def head_mask(h, width):
@@ -304,11 +320,11 @@
     m["o_bs"][...] = (acc / total).astype(BF16)
     m["l_bs"][...] = peak + jnp.log2(total)
 
-    def combine(tag, copies):
-        for copy in copies:
-            copy.wait_recv()
+    def combine(tag, groups):
+        for group in groups:
+            group.wait_recv()
         slots = "b" if tag == "bs" else "c"
-        size = len(copies) // 2
+        size = m["o_" + slots].shape[0]
         logs = [m["l_" + tag][...]] + [m["l_" + slots][n] for n in range(size)]
         peak = functools.reduce(jnp.maximum, logs)
         shares = [jnp.exp2(x - peak) for x in logs]
@@ -318,24 +334,36 @@
             acc = acc + m["o_" + slots][n].astype(F32) * shares[n + 1]
         return acc / total, peak + jnp.log2(total)
 
-    ob = to_all(m["o_bs"], m["o_b"], group_n) + to_all(m["l_bs"], m["l_b"], group_n)
-
-    for copy in kve:
-        copy.wait_recv()
+    ob = [to_all(m["o_bs"], m["o_b"], group_n), to_all(m["l_bs"], m["l_b"], group_n)]
+
+    mine = m["kv_full"].at[part_of(j, ch), part_of(zn, piece)]
+    m["kv_full"][part_of(j, ch), part_of(zn, piece)] = gather(m["kv_cs"][...], kvc, m["kv_c"])
+    kve = send_all([(mine, mine, dev) for dev in group_n], m["kv_b"])
+    partners_next = [
+        plan(m[name].at[pl.ds(8 - 8 * c, 2)], m[name].at[pl.ds(6 - 4 * c, 2)], partner)
+        for name in ("kx", "vx")
+    ]
+    beside += partners_next
+    inner = (z > 0) & (z < z_n - 1)
+
+    def pass_on():
+        for copy in window:
+            copy.wait_recv()
+        for copy in partners_next:
+            copy.start()
+
+    pl.when(inner)(pass_on)
+
+    kve.wait_recv()
     mine = m["kv_full"].at[part_of(j, ch), :]
-    kvd = [send(mine, mine, dev) for dev in group_j]
+    kvd = send_all([(mine, mine, dev) for dev in group_j], m["kv_a"])
 
     o, l = combine("bs", ob)
     m["o_cs"][...] = o.astype(BF16)
     m["l_cs"][...] = l
-    oc = to_all(m["o_cs"], m["o_c"], group_f) + to_all(m["l_cs"], m["l_c"], group_f)
-
-    for copy in window:
-        copy.wait_recv()
-    for name in ("kx", "vx"):
-        beside.append(
-            send(m[name].at[pl.ds(8 - 8 * c, 2)], m[name].at[pl.ds(6 - 4 * c, 2)], partner)
-        )
+    oc = [to_all(m["o_cs"], m["o_c"], group_f), to_all(m["l_cs"], m["l_c"], group_f)]
+
+    pl.when(jnp.logical_not(inner))(pass_on)
     loads["rand"].wait()
     for copy in beside:
         copy.wait_recv()
@@ -381,8 +409,7 @@
     for step in range(4):
         attend_near(step, 0)
 
-    for copy in kvd:
-        copy.wait_recv()
+    kvd.wait_recv()
     gv_t = m["kv_full"][:, FEATS:].astype(F32).T.astype(BF16)
     for b in range(2):
         m["gvt"][b] = gv_t[:, b * BLOCK : (b + 1) * BLOCK]
@@ -419,21 +446,18 @@
     o_t = jnp.concatenate([o_t[:qc], o_t[qc:]], axis=1).astype(BF16)
     m["o_full"][part_of(y, qc), part_of(c, half)] = o_t
     mine = m["o_full"].at[part_of(y, qc), part_of(c, half)]
-    od = [send(mine, mine, dev) for dev in group_j]
-    for copy in od:
-        copy.wait_recv()
+    od = send_all([(mine, mine, dev) for dev in group_j], m["q_a"])
+    od.wait_recv()
 
     placed = dot_nn(m["pick"][...], m["o_full"][...])
     m["att"][...] = (placed + m["attl"][...]).astype(BF16)
     per = TOK // heads
-    ax = [
-        send(m["att"].at[part_of((hd + d + 1) % heads, per)], m["asl"].at[d], group_h[d])
-        for d in range(heads - 1)
-    ]
+    pieces = [m["att"].at[part_of((hd + d) % heads, per)] for d in range(1, heads)]
+    ax = send_all([(src, m["asl"].at[d], group_h[d]) for d, src in enumerate(pieces)], m["asl"])
     mixed = dot_nn(m["att"][part_of(hd, per)], m["osl"][0])
+    ow.wait_recv()
+    ax.wait_recv()
     for d in range(heads - 1):
-        ow[d].wait_recv()
-        ax[d].wait_recv()
         mixed = mixed + dot_nn(m["asl"][d], m["osl"][d + 1])
     out_v[...] = mixed.astype(BF16)
     for copy in started:
@@ -463,8 +487,8 @@
         k_weight,
         v_weight,
         o_weight,
-        rand_blocks,
-        global_pos.reshape(1, GLOBALS),
+        pltpu.with_memory_space_constraint(rand_blocks, pltpu.HBM),
+        pltpu.with_memory_space_constraint(global_pos.reshape(1, GLOBALS), pltpu.HBM),
     )
 
 

time: 58.3 us -> 54.6 us (0.937)
  Pallas kernels: 56.1 us -> 53.8 us
  local copies, waits for them, and re-layouts: 2.01 us -> 0.66 us
    pallas_call x1, Pallas kernels: 56.1 us -> 53.8 us  [shards_fn(): pl.pallas_call(functools.partial(kernel, split, heads, list(scratch)), ou...]
    unnamed x5 -> x1, local copies, waits for them, and re-layouts: 2.01 us -> 0.66 us
where the time goes in v4:
time: 54.6 us; the launch traced here: 54.4 us
  Pallas kernels  53.8 us (99%)
  local copies, waits for them, and re-layouts  0.66 us (1%)
    pallas_call x1, Pallas kernels, shards_fn(): pl.pallas_call(functools.partial(kernel, split, heads, list(scratch)), ou...  53.8 us

profile of v4, /device:TPU:1, one launch (start us, length us, event | category | flops | bytes accessed | tf_op | source)
XLA Modules:
  0.0 54.4 jit_solution(3891328578808869698)
XLA Ops:
  0.0 53.8 %layer.1 = bf16[64,1024]{1,0:T(8,128)(2,1)S(1)} custom-call(bf16[256,1024]{1,0:T(8,128)(2,1)} %tok_h.1, bf16[1024,256]{1,0:T(8,128)(2,1)} %wq_h.1, bf16[1024,256]{1,0:T(8,128)(2,1)} %wk_h.1, bf16[1024,256]{1,0:T(8,128)(2,1)} %wv_h.1, bf16[256,1024]{1,0:T(8,128)(2,1)} %ow_h.1, s32[2,3]{1,0:T(2,128)} %rand_h.1, s32[1,256]{1,0:T(1,128)} %bitcast.1), custom_call_target="tpu_custom_call" | custom-call | tf_op jit(solution)/shard_map/layer/pallas_call | solution.py:474
  53.8 0.7 %copy.9 = bf16[64,1024]{1,0:T(8,128)(2,1)} copy(bf16[64,1024]{1,0:T(8,128)(2,1)S(1)} %layer.1) | data formatting | bytes 262144

commit v5 on v4

--- a/solution.py
+++ b/solution.py
@@ -45,9 +45,8 @@
 def scratch_of(split, heads, d):
     y_n, zn_n, zf_n = split
     r = 2 * y_n
-    ch = GLOBALS // r
     qc = GLOBALS // y_n
-    piece = 2 * FEATS // zn_n
+    piece = qc // zn_n
     vm = pltpu.VMEM
     out = {
         "tok": vm((TOK, d), BF16),
@@ -78,11 +77,14 @@
         "q_cs": vm((qc, 2 * HEAD_DIM), BF16),
         "q_c": vm((zf_n - 1, qc, 2 * HEAD_DIM), BF16),
         "kv_part": vm((GLOBALS, 2 * FEATS), BF16),
-        "kv_a": vm((r - 1, ch, 2 * FEATS), BF16),
-        "kv_bs": vm((ch, 2 * FEATS), BF16),
-        "kv_b": vm((zn_n - 1, ch, piece), BF16),
-        "kv_cs": vm((ch, piece), BF16),
-        "kv_c": vm((zf_n - 1, ch, piece), BF16),
+        "kv_p": vm((GLOBALS, FEATS), BF16),
+        "kv_ps": vm((GLOBALS, FEATS), BF16),
+        "kv_a": vm((y_n - 1, qc, FEATS), BF16),
+        "kv_bs": vm((qc, FEATS), BF16),
+        "kv_b": vm((zn_n - 1, piece, FEATS), BF16),
+        "kv_cs": vm((piece, FEATS), BF16),
+        "kv_c": vm((zf_n - 1, piece, FEATS), BF16),
+        "kv_size": vm((r - 1, qc, FEATS), BF16),
         "kv_full": vm((GLOBALS, 2 * FEATS), BF16),
         "o_bs": vm((HEAD_DIM, 2 * qc), BF16),
         "o_b": vm((zn_n - 1, HEAD_DIM, 2 * qc), BF16),
@@ -96,7 +98,7 @@
         "grow": vm((1, GLOBALS), jnp.int32),
         "rand": pltpu.SMEM((2, RAND), jnp.int32),
     }
-    copies = 31
+    copies = 31 + heads - 1
     out["send"] = pltpu.SemaphoreType.DMA((copies,))
     out["recv"] = pltpu.SemaphoreType.DMA((copies,))
     out["greet"] = pltpu.SemaphoreType.REGULAR
@@ -108,21 +110,21 @@
     m = dict(zip(names, scratch))
     y_n, zn_n, zf_n = split
     r = 2 * y_n
-    ch = GLOBALS // r
     qc = GLOBALS // y_n
-    piece = 2 * FEATS // zn_n
+    piece = qc // zn_n
     half = 2 * HEAD_DIM
     shards = r * zn_n * zf_n
     z_n = zn_n * zf_n
     tm = lax.axis_index("tm")
     hd = lax.axis_index("head")
 
-    order = (("grow", grow_h), ("tok", tok_h), ("wq", wq_h), ("wk", wk_h), ("wv", wv_h))
+    order = (("tok", tok_h), ("wq", wq_h), ("grow", grow_h), ("wk", wk_h), ("wv", wv_h))
     order += (("osl", ow_h), ("rand", rand_h))
     loads = {}
     for i, (name, src) in enumerate(order):
         dst = m[name].at[0] if name == "osl" else m[name]
         loads[name] = pltpu.make_async_copy(src, dst, m["load"].at[i])
+    for name in ("tok", "wq", "grow"):
         loads[name].start()
 
     y = tm // (2 * z_n)
@@ -151,11 +153,13 @@
     group_w = [((tm + d + shards) % shards, hd) for d in steps_w]
     next_f = [dev for d, dev in zip(far_steps, group_f) if min(d, zf_n - d) == 1]
     relayed = len(next_f) < len(group_f)
-    everyone = group_j + group_n + next_f + group_h + group_w
+    everyone = next_f + group_n + group_w + group_j + group_h
 
     barrier = pltpu.get_barrier_semaphore()
     for dev in everyone:
         pl.semaphore_signal(barrier, inc=1, device_id=dev, device_id_type=MESH)
+    for name in ("wk", "wv", "osl", "rand"):
+        loads[name].start()
 
     count = [0]
     started = []
@@ -233,8 +237,7 @@
     loads["wv"].wait()
     v32 = dot_nn(m["tok"][...], m["wv"][...])
     m["kv_part"][:, FEATS:] = dot_nn(pick_t, v32.astype(BF16)).astype(BF16)
-    pieces = [m["kv_part"].at[part_of(yy * 2 + cc, ch)] for yy, cc in there]
-    kva = send_all([(src, m["kv_a"].at[n], group_j[n]) for n, src in enumerate(pieces)], m["kv_a"])
+    kvp = send(m["kv_part"].at[:, part_of(1 - c, FEATS)], m["kv_p"], partner)
     v_t = v32.T.astype(BF16)
     for b in range(2):
         m["vx"][4 + b] = v_t[:, b * BLOCK : (b + 1) * BLOCK]
@@ -262,6 +265,18 @@
         m["kg"][0, b] = m["kx"][4 + b, :, part_of(c, half)]
         m["vg"][0, b] = m["vx"][4 + b, part_of(c, half), :]
 
+    kvp.wait_recv()
+    m["kv_ps"][...] = (
+        m["kv_part"][:, part_of(c, FEATS)].astype(F32) + m["kv_p"][...].astype(F32)
+    ).astype(BF16)
+    same = [n for n, step in enumerate(steps_j) if step[1] == 0]
+    kva = send_all(
+        [
+            (m["kv_ps"].at[part_of(there[n][0], qc)], m["kv_a"].at[i], group_j[n])
+            for i, n in enumerate(same)
+        ],
+        m["kv_a"],
+    )
     m["q_bs"][...] = gather(m["q_part"][part_of(y, qc), part_of(c, half)], qa, m["q_a"])
     qb = to_all(m["q_bs"], m["q_b"], group_n)
     kvg = {}
@@ -278,20 +293,21 @@
                 [(way[i][0], m[name].at[slots[i]], group_j[n]) for i, n in enumerate(at)],
                 m[name].at[pl.ds(0, len(at))],
             )
-    m["kv_bs"][...] = gather(m["kv_part"][part_of(j, ch), :], kva, m["kv_a"])
-    pieces = [m["kv_bs"].at[:, part_of(at, piece)] for at in near]
+    m["kv_bs"][...] = gather(m["kv_ps"][part_of(y, qc), :], kva, m["kv_a"])
+    pieces = [m["kv_bs"].at[part_of(at, piece)] for at in near]
     kvb = send_all([(src, m["kv_b"].at[n], group_n[n]) for n, src in enumerate(pieces)], m["kv_b"])
     m["q_cs"][...] = gather(m["q_bs"][...], qb, m["q_b"])
     if relayed:
         pl.semaphore_wait(m["greet"], len(next_f))
     qcs = to_all(m["q_cs"], m["q_c"], group_f)
-    m["kv_cs"][...] = gather(m["kv_bs"][:, part_of(zn, piece)], kvb, m["kv_b"])
-    kvc = to_all(m["kv_cs"], m["kv_c"], group_f)
-    start_window(window[2:], False)
     kvg.pop(("kg", 1)).wait_recv()
     forward = [send(m["kg"].at[pl.ds(6, 2)], m["kg"].at[pl.ds(4, 2)], group_j[2])]
     kvg.pop(("vg", 3)).wait_recv()
     forward += [send(m["vg"].at[pl.ds(2, 2)], m["vg"].at[pl.ds(4, 2)], group_j[4])]
+
+    m["kv_cs"][...] = gather(m["kv_bs"][part_of(zn, piece), :], kvb, m["kv_b"])
+    kvc = to_all(m["kv_cs"], m["kv_c"], group_f)
+    start_window(window[2:], False)
     gq = gather(m["q_cs"][...], qcs, m["q_c"])
     start_window(window, True)
     for copy in list(kvg.values()) + forward:
@@ -336,8 +352,8 @@
 
     ob = [to_all(m["o_bs"], m["o_b"], group_n), to_all(m["l_bs"], m["l_b"], group_n)]
 
-    mine = m["kv_full"].at[part_of(j, ch), part_of(zn, piece)]
-    m["kv_full"][part_of(j, ch), part_of(zn, piece)] = gather(m["kv_cs"][...], kvc, m["kv_c"])
+    mine = m["kv_full"].at[part_of(y * zn_n + zn, piece), part_of(c, FEATS)]
+    m["kv_full"][part_of(y * zn_n + zn, piece), part_of(c, FEATS)] = gather(m["kv_cs"][...], kvc, m["kv_c"])
     kve = send_all([(mine, mine, dev) for dev in group_n], m["kv_b"])
     partners_next = [
         plan(m[name].at[pl.ds(8 - 8 * c, 2)], m[name].at[pl.ds(6 - 4 * c, 2)], partner)
@@ -347,22 +363,21 @@
     inner = (z > 0) & (z < z_n - 1)
 
     def pass_on():
-        for copy in window:
-            copy.wait_recv()
-        for copy in partners_next:
+        for n, copy in enumerate(partners_next):
+            for arriving in window[2 * n : 2 * n + 2]:
+                arriving.wait_recv()
             copy.start()
 
     pl.when(inner)(pass_on)
-
-    kve.wait_recv()
-    mine = m["kv_full"].at[part_of(j, ch), :]
-    kvd = send_all([(mine, mine, dev) for dev in group_j], m["kv_a"])
 
     o, l = combine("bs", ob)
     m["o_cs"][...] = o.astype(BF16)
     m["l_cs"][...] = l
     oc = [to_all(m["o_cs"], m["o_c"], group_f), to_all(m["l_cs"], m["l_c"], group_f)]
 
+    kve.wait_recv()
+    mine = m["kv_full"].at[part_of(y, qc), part_of(c, FEATS)]
+    kvd = send_all([(mine, mine, dev) for dev in group_j], m["kv_size"])
     pl.when(jnp.logical_not(inner))(pass_on)
     loads["rand"].wait()
     for copy in beside:
@@ -397,10 +412,14 @@
             peak = top if peak is None else jnp.maximum(peak, top)
         total = jnp.zeros((1, 2 * BLOCK), F32)
         acc = jnp.zeros((half, 2 * BLOCK), F32)
-        for n in range(7):
-            e = jnp.exp2(m["s"][n] - peak)
-            total = total + jnp.sum(e, axis=0, keepdims=True)
-            acc = acc + dot_nn(m["vx"][spots_x[n], feats, :], e.astype(BF16))
+        for at in ((0, 1), (2, 3), (4, 5), (6,)):
+            weights, values = [], []
+            for n in at:
+                e = jnp.exp2(m["s"][n] - peak)
+                total = total + jnp.sum(e, axis=0, keepdims=True)
+                weights.append(e.astype(BF16))
+                values.append(m["vx"][spots_x[n], feats, :])
+            acc = acc + dot_nn(jnp.concatenate(values, axis=1), jnp.concatenate(weights, axis=0))
         m["peak"][step] = peak
         m["total"][step] = total
         m["acc"][step] = acc
@@ -427,8 +446,7 @@
         total = m["total"][step] * share + jnp.sum(e, axis=0, keepdims=True)
         e = e.astype(BF16)
         acc = m["acc"][step] * share
-        for b in range(2):
-            acc = acc + dot_nn(m["gvt"][b, feats, :], e[b * BLOCK : (b + 1) * BLOCK])
+        acc = acc + dot_nn(jnp.concatenate([m["gvt"][b, feats, :] for b in range(2)], axis=1), e)
         acc = acc / total
         for n in range(2):
             m["att_t"][part_of(pair * 2 + n, HEAD_DIM), part_of(jb, BLOCK)] = acc[
@@ -452,13 +470,16 @@
     placed = dot_nn(m["pick"][...], m["o_full"][...])
     m["att"][...] = (placed + m["attl"][...]).astype(BF16)
     per = TOK // heads
-    pieces = [m["att"].at[part_of((hd + d) % heads, per)] for d in range(1, heads)]
-    ax = send_all([(src, m["asl"].at[d], group_h[d]) for d, src in enumerate(pieces)], m["asl"])
+    x_steps = sorted(range(1, heads), key=lambda d: -min(d, heads - d))
+    ax = {
+        d: send(m["att"].at[part_of((hd + d) % heads, per)], m["asl"].at[d - 1], group_h[d - 1])
+        for d in x_steps
+    }
     mixed = dot_nn(m["att"][part_of(hd, per)], m["osl"][0])
     ow.wait_recv()
-    ax.wait_recv()
-    for d in range(heads - 1):
-        mixed = mixed + dot_nn(m["asl"][d], m["osl"][d + 1])
+    for d in x_steps[::-1]:
+        ax[d].wait_recv()
+        mixed = mixed + dot_nn(m["asl"][d - 1], m["osl"][d])
     out_v[...] = mixed.astype(BF16)
     for copy in started:
         copy.wait_send()

time: 54.6 us -> 52.8 us (0.967)
  Pallas kernels: 53.8 us -> 52 us
    pallas_call x1, Pallas kernels: 53.8 us -> 52 us  [shards_fn(): pl.pallas_call(functools.partial(kernel, split, heads, list(scratch)), ou...]
where the time goes in v5:
time: 52.8 us; the launch traced here: 52.7 us
  Pallas kernels  52 us (98%)
  local copies, waits for them, and re-layouts  0.66 us (1%)
    pallas_call x1, Pallas kernels, shards_fn(): pl.pallas_call(functools.partial(kernel, split, heads, list(scratch)), ou...  52 us

profile of v5, /device:TPU:1, one launch (start us, length us, event | category | flops | bytes accessed | tf_op | source)
XLA Modules:
  0.0 52.7 jit_solution(6498129261070649716)
XLA Ops:
  0.0 52.0 %layer.1 = bf16[64,1024]{1,0:T(8,128)(2,1)S(1)} custom-call(bf16[256,1024]{1,0:T(8,128)(2,1)} %tok_h.1, bf16[1024,256]{1,0:T(8,128)(2,1)} %wq_h.1, bf16[1024,256]{1,0:T(8,128)(2,1)} %wk_h.1, bf16[1024,256]{1,0:T(8,128)(2,1)} %wv_h.1, bf16[256,1024]{1,0:T(8,128)(2,1)} %ow_h.1, s32[2,3]{1,0:T(2,128)} %rand_h.1, s32[1,256]{1,0:T(1,128)} %bitcast.1), custom_call_target="tpu_custom_call" | custom-call | tf_op jit(solution)/shard_map/layer/pallas_call | solution.py:495
  52.0 0.7 %copy.9 = bf16[64,1024]{1,0:T(8,128)(2,1)} copy(bf16[64,1024]{1,0:T(8,128)(2,1)S(1)} %layer.1) | data formatting | bytes 262144

commit v6 on v5

--- a/solution.py
+++ b/solution.py
@@ -251,11 +251,17 @@
             window.append(plan(own, m[name].at[pl.ds(2 * (SPREAD - step), 2)], dev))
         beside.append(send(own, m[name].at[pl.ds(2 + 4 * c, 2)], partner))
 
-    def start_window(copies, at_edge):
+    def start_window(copies):
         for n, copy in enumerate(copies):
-            pl.when(edges[n % 2] if at_edge else jnp.logical_not(edges[n % 2]))(copy.start)
-
-    start_window(window[:2], False)
+            pl.when(jnp.logical_not(edges[n % 2]))(copy.start)
+
+    def start_edge(ahead):
+        for n, copy in enumerate(window):
+            first = c == (n + 1) % 2
+            turn = first if ahead else jnp.logical_not(first)
+            pl.when(edges[n % 2] & turn)(copy.start)
+
+    start_window(window[:2])
     loads["osl"].wait()
     ow = send_all(
         [(m["osl"].at[0], m["osl"].at[d + 1], dev) for d, dev in enumerate(group_h)],
@@ -307,11 +313,12 @@
 
     m["kv_cs"][...] = gather(m["kv_bs"][part_of(zn, piece), :], kvb, m["kv_b"])
     kvc = to_all(m["kv_cs"], m["kv_c"], group_f)
-    start_window(window[2:], False)
+    start_window(window[2:])
     gq = gather(m["q_cs"][...], qcs, m["q_c"])
-    start_window(window, True)
+    start_edge(True)
     for copy in list(kvg.values()) + forward:
         copy.wait_recv()
+    start_edge(False)
 
     def head_mask(h, width):
         lane_head = lax.broadcasted_iota(jnp.int32, (1, width), 1) // HEAD_DIM

time: 52.8 us -> 52.8 us (level)
  no operation moved by 1% of the time
where the time goes in v6:
time: 52.8 us; the launch traced here: 52.7 us
  Pallas kernels  52 us (98%)
  local copies, waits for them, and re-layouts  0.66 us (1%)
    pallas_call x1, Pallas kernels, shards_fn(): pl.pallas_call(functools.partial(kernel, split, heads, list(scratch)), ou...  52 us

profile of v6, /device:TPU:1, one launch (start us, length us, event | category | flops | bytes accessed | tf_op | source)
XLA Modules:
  0.0 52.7 jit_solution(16792979668623150156)
XLA Ops:
  0.0 52.0 %layer.1 = bf16[64,1024]{1,0:T(8,128)(2,1)S(1)} custom-call(bf16[256,1024]{1,0:T(8,128)(2,1)} %tok_h.1, bf16[1024,256]{1,0:T(8,128)(2,1)} %wq_h.1, bf16[1024,256]{1,0:T(8,128)(2,1)} %wk_h.1, bf16[1024,256]{1,0:T(8,128)(2,1)} %wv_h.1, bf16[256,1024]{1,0:T(8,128)(2,1)} %ow_h.1, s32[2,3]{1,0:T(2,128)} %rand_h.1, s32[1,256]{1,0:T(1,128)} %bitcast.1), custom_call_target="tpu_custom_call" | custom-call | tf_op jit(solution)/shard_map/layer/pallas_call | solution.py:502
  52.0 0.7 %copy.9 = bf16[64,1024]{1,0:T(8,128)(2,1)} copy(bf16[64,1024]{1,0:T(8,128)(2,1)S(1)} %layer.1) | data formatting | bytes 262144
